TPU v7x, 512 devices: a whole 4x4x16 slice. The times are simulated.
512 devices in a mesh: band: 128 (over z, y, core), batch: 4 (over x).
Axes of the slice: x: 4, y: 4, z: 16, core: 2. Of those that a mesh axis runs over, the one named last changes fastest.
Arguments:
- tiles: bfloat16 [128, 128, 128, 128], P('band'), may hold values from -256 to 256, as said below
- tile_row: int32 [128, 128], P('band'), may hold values from 0 to 3, as said below
- tile_col: int32 [128, 128], P('band'), may hold values from 0 to 255, as said below
- tile_count: int32 [128], P('band'), may hold values from 80 to 128, as said below
- cost: float32 [8, 32768], P('batch', 'band'), may hold values from -6 to 6
- bound_vec: float32 [65536], P('band'), may hold values from -6 to 6
- x_start: float32 [8, 32768], P('batch', 'band'), may hold values from 0 to 1
- y_start: float32 [8, 65536], P('batch', 'band'), may hold values from 0 to 1
Outputs:
- x_out: float32 [8, 32768], P('batch', 'band')
- y_out: float32 [8, 65536], P('batch', 'band')
Inputs may be any that keep to these rules, and one draw needn't show every extreme that they name: `tile_row`: within a band, tiles 0 to 3 lie in row blocks 0 to 3 in order. `tile_col`: the owner of column block k is band k // 2. Among a band's live tiles at most 2 have one owner, and the tiles of one owner stand in a row; tiles 0 to 1 of band b lie in column blocks b * 2 + t, so each band gives exactly 2 tiles to its own owner and every row block and column block holds a live tile. `tile_count`: one band in every draw is full. `tiles`: every entry has magnitude 0.1 or more.
All inputs are finite; a program needn't handle non-finite values.
Results may differ from a plain program's by a relative error of at most 0.0003.
Values sent between devices are 32-bit elements; how exact they have to be, the bound alone decides.
A program may use at most 64 MiB of HBM per device.

v0:
```python
import jax
import jax.numpy as jnp
from jax import lax
from jax.sharding import PartitionSpec as P

ROWBLK = 4
COLBLK = 2


step_size = 0.0625
high = lax.Precision.HIGHEST


def row_peak_of(magnitude, select):
    row_max = jnp.max(magnitude, axis=2)
    return jnp.max(jnp.where(select[:, :, None], row_max[None], 0.0), axis=1)


def col_peak_of(magnitude, tile_rows, alive, slot_of, rscale, overflow):
    spread = rscale[tile_rows]
    peak = jnp.max(magnitude * spread[:, :, None], axis=1)
    peak = jnp.where(alive[:, None], peak, 0.0)
    return jnp.zeros((overflow, magnitude.shape[2]), jnp.float32).at[slot_of].max(peak, mode="drop")


def shards(tiles, tile_row, tile_col, tile_count, cost, bound_vec, x_start, y_start):
    blocks = tiles[0]
    tile_rows = tile_row[0]
    tile_cols = tile_col[0]
    live_count = tile_count[0]
    ntile = blocks.shape[0]
    tile_edge = blocks.shape[1]
    band_count = lax.axis_size("band")
    own_band = lax.axis_index("band")
    capacity = max(2, 2 * ntile // band_count)
    overflow = band_count * capacity
    indices = jnp.arange(ntile, dtype=jnp.int32)
    live = indices < live_count
    owner_of = tile_cols // COLBLK
    earlier = (
        (owner_of[:, None] == owner_of[None, :])
        & live[None, :]
        & (indices[None, :] < indices[:, None])
    )
    rank_in = jnp.sum(earlier.astype(jnp.int32), axis=1)
    slot_of = jnp.where(live, owner_of * capacity + rank_in, overflow)
    requests = (
        jnp.full((overflow,), -1, jnp.int32)
        .at[slot_of]
        .set(tile_cols, mode="drop")
        .reshape(band_count, capacity)
    )
    rowsel = (tile_rows[None, :] == jnp.arange(ROWBLK, dtype=jnp.int32)[:, None]) & live[None, :]
    rowsel_f = rowsel.astype(jnp.float32)
    widened = blocks.astype(jnp.float32)
    magnitude = jnp.abs(widened)
    quarter = ntile // lax.axis_size("batch")
    offset = lax.axis_index("batch") * quarter
    part_mag = lax.dynamic_slice_in_dim(magnitude, offset, quarter, 0)
    part_rows = lax.dynamic_slice_in_dim(tile_rows, offset, quarter, 0)
    part_live = lax.dynamic_slice_in_dim(live, offset, quarter, 0)
    part_slot = lax.dynamic_slice_in_dim(slot_of, offset, quarter, 0)
    part_sel = lax.dynamic_slice_in_dim(rowsel, offset, quarter, 1)
    row_peak = lax.pmax(row_peak_of(part_mag, part_sel), "batch")
    rscale = lax.rsqrt(row_peak)
    col_send = col_peak_of(part_mag, part_rows, part_live, part_slot, rscale, overflow)
    col_send = lax.pmax(col_send, "batch")
    got_ids, got_max = (
        lax.all_to_all(requests, "band", split_axis=0, concat_axis=0, tiled=True),
        lax.all_to_all(
            col_send.reshape(band_count, capacity, tile_edge),
            "band",
            split_axis=0,
            concat_axis=0,
            tiled=True,
        ),
    )
    local_id = got_ids - own_band * COLBLK
    owned = local_id[:, :, None] == jnp.arange(COLBLK, dtype=jnp.int32)[None, None, :]
    col_peak = jnp.max(jnp.where(owned[..., None], got_max[:, :, None, :], 0.0), axis=(0, 1))
    cscale = lax.rsqrt(col_peak).reshape(-1)
    rflat = rscale.reshape(-1)
    owned_f = owned.astype(jnp.float32)
    fetch_at = jnp.minimum(slot_of, overflow - 1)

    def forward(vec):
        columns = vec.shape[0]
        scaled = vec * cscale
        replies = jnp.einsum(
            "asc,kcj->askj", owned_f, scaled.reshape(columns, COLBLK, tile_edge), precision=high
        )
        returned = lax.all_to_all(replies, "band", split_axis=0, concat_axis=0, tiled=True).reshape(
            overflow, columns, tile_edge
        )
        picked = jnp.take(returned, fetch_at, axis=0)
        product = jnp.einsum("tij,tkj->tki", widened, picked, precision=high)
        product = jnp.where(live[:, None, None], product, 0.0)
        return (
            jnp.einsum("rt,tki->kri", rowsel_f, product, precision=high).reshape(columns, -1)
            * rflat
        )

    def adjoint(vec):
        columns = vec.shape[0]
        weighted = (vec * rflat).reshape(columns, ROWBLK, tile_edge)
        spread = jnp.einsum("rt,kri->tki", rowsel_f, weighted, precision=high)
        partial_value = jnp.einsum("tij,tki->tkj", widened, spread, precision=high)
        outgoing = (
            jnp.zeros((overflow, columns, tile_edge), jnp.float32)
            .at[slot_of]
            .add(partial_value, mode="drop")
        )
        incoming = lax.all_to_all(
            outgoing.reshape(band_count, capacity, columns, tile_edge),
            "band",
            split_axis=0,
            concat_axis=0,
            tiled=True,
        )
        summed = jnp.einsum("asc,askj->kcj", owned_f, incoming, precision=high)
        return summed.reshape(columns, -1) * cscale

    scost = cost * cscale
    sbound = bound_vec * rflat
    primal_one = jnp.maximum(0.0, x_start - step_size * (scost - adjoint(y_start)))
    dual_one = jnp.maximum(
        0.0, y_start + step_size * (sbound - forward(2.0 * primal_one - x_start))
    )
    primal_step = jnp.sum((primal_one - x_start) ** 2, axis=1, keepdims=True)
    dual_step = jnp.sum((dual_one - y_start) ** 2, axis=1, keepdims=True)
    primal_step, dual_step = lax.psum((primal_step, dual_step), "band")
    weight_ratio = jnp.sqrt((dual_step + 1e-06) / (primal_step + 1e-06))
    primal_two = jnp.maximum(
        0.0, primal_one - step_size / weight_ratio * (scost - adjoint(dual_one))
    )
    dual_two = jnp.maximum(
        0.0, dual_one + step_size * weight_ratio * (sbound - forward(2.0 * primal_two - primal_one))
    )
    return (primal_two, dual_two)


def solution(mesh):
    return jax.shard_map(
        shards,
        mesh=mesh,
        in_specs=(
            P("band", None, None, None),
            P("band", None),
            P("band", None),
            P("band"),
            P("batch", "band"),
            P("band"),
            P("batch", "band"),
            P("batch", "band"),
        ),
        out_specs=(P("batch", "band"), P("batch", "band")),
        check_vma=False,
    )
```

profile of v0, /device:TPU:1, one launch (start us, length us, event | category | flops | bytes accessed | tf_op | source)
XLA Modules:
  0.0 538.1 jit_solution(12446176027909140843)
XLA Ops:
  9.3 0.7 fusion.55
  10.0 1.1 scatter_custom_fusion
  11.1 0.8 all_to_all.21
  11.9 20.6 %all-to-all-start = ((s32[128,1,2]{2,1,0:T(1,128)}), s32[128,1,2]{2,1,0:T(1,128)S(1)}, u32[]{:S(2)}, u32[]{:S(2)}) async-start(s32[128,1,2]{2,1,0:T(1,128)} %bitcast.6), calls=%async_computation | async-start | bytes 131072 | tf_op jit(solution)/shard_map/all_to_all | solution.py:69
  32.6 0.7 fusion.56
  34.8 1.6 fusion
  36.5 9.1 %pmax.14 = f32[4,128]{1,0:T(4,128)S(1)} all-reduce(f32[4,128]{1,0:T(4,128)S(1)} %select_reduce_fusion.1), channel_id=1, replica_groups=mesh['band'=128,'batch'=4] {'batch'}, use_global_device_ids=true, to_apply=%region_4.5 | all-reduce | flops 512 | bytes 4096 | tf_op jit(solution)/shard_map/pmax | solution.py:64
  46.2 1.7 multiply_reduce_fusion
  47.9 1.4 scatter_custom_fusion.1
  49.3 0.7 broadcast_multiply_fusion.1
  50.1 54.1 %all-reduce.3.cloned.1.call-done = f32[128,2,128]{2,1,0:T(2,128)} async-done(((f32[128,2,128]{2,1,0:T(2,128)}), f32[128,2,128]{2,1,0:T(2,128)}) %all-reduce.3.cloned.1.call-update) | async-done | bytes 131088 | tf_op jit(solution)/shard_map/pmax | solution.py:67
  104.1 18.7 %all-to-all-start.1 = ((f32[128,2,128]{2,1,0:T(2,128)}), f32[128,2,128]{2,1,0:T(2,128)S(1)}, u32[]{:S(2)}, u32[]{:S(2)}) async-start(f32[128,2,128]{2,1,0:T(2,128)} %all-reduce.3.cloned.1.call-done), calls=%async_computation.1 | async-start | bytes 262144 | tf_op jit(solution)/shard_map/all_to_all | solution.py:70
  123.1 5.1 fusion.7
  128.3 5.0 scatter_fusion
  133.3 0.8 copy.73
  134.1 4.8 all-to-all-done.1
  138.9 11.3 %all-to-all-start.2 = ((f32[128,2,2,128]{3,1,2,0:T(2,128)}), f32[128,2,2,128]{3,1,2,0:T(2,128)S(1)}, u32[]{:S(2)}, u32[]{:S(2)}) async-start(f32[128,2,2,128]{3,1,2,0:T(2,128)} %copy.73), calls=%async_computation.2 | async-start | bytes 524288 | tf_op jit(solution)/shard_map/all_to_all | solution.py:113
  150.5 20.2 %all-to-all-done.2 = f32[128,2,2,128]{3,1,2,0:T(2,128)S(1)} async-done(((f32[128,2,2,128]{3,1,2,0:T(2,128)}), f32[128,2,2,128]{3,1,2,0:T(2,128)S(1)}, u32[]{:S(2)}, u32[]{:S(2)}) %all-to-all-start.2) | async-done | bytes 262176 | tf_op jit(solution)/shard_map/all_to_all | solution.py:113
  171.4 0.9 copy.75
  172.3 8.3 %all-to-all-start.3 = ((f32[128,2,2,128]{3,2,1,0:T(2,128)}), f32[128,2,2,128]{3,2,1,0:T(2,128)S(1)}, u32[]{:S(2)}, u32[]{:S(2)}) async-start(f32[128,2,2,128]{3,2,1,0:T(2,128)} %copy.75), calls=%async_computation.3 | async-start | bytes 524288 | tf_op jit(solution)/shard_map/all_to_all | solution.py:92
  180.6 20.4 %all-to-all-done.3 = f32[128,2,2,128]{3,2,1,0:T(2,128)S(1)} async-done(((f32[128,2,2,128]{3,2,1,0:T(2,128)}), f32[128,2,2,128]{3,2,1,0:T(2,128)S(1)}, u32[]{:S(2)}, u32[]{:S(2)}) %all-to-all-start.3) | async-done | bytes 262176 | tf_op jit(solution)/shard_map/all_to_all | solution.py:92
  201.1 0.7 gather_fusion.1
  201.8 8.4 %convolution_select_fusion.1 = f32[128,2,128]{2,1,0:T(2,128)S(1)} fusion(f32[128,2,128]{2,1,0:T(2,128)S(1)} %gather_fusion.1, pred[128]{0:T(512)(128)(4,1)S(1)} %get-tuple-element.13, pred[128]{0:T(512)(128)(4,1)S(1)} %iota_compare_fusion.3, bf16[1,128,128,128]{3,2,1,0:T(8,128)(2,1)} %param.10), kind=kOutput, calls=%fused_computation.11 | convolution fusion | flops 50397184 | bytes 4456704 | tf_op jit(solution)/shard_map/tij,tkj->tki/dot_general | solution.py:96
  210.8 5.1 fusion.4
  215.9 5.0 scatter_fusion.1
  221.0 0.8 copy.81
  221.8 8.3 %all-to-all-start.4 = ((f32[128,2,2,128]{3,1,2,0:T(2,128)}), f32[128,2,2,128]{3,1,2,0:T(2,128)S(1)}, u32[]{:S(2)}, u32[]{:S(2)}) async-start(f32[128,2,2,128]{3,1,2,0:T(2,128)} %copy.81), calls=%async_computation.4 | async-start | bytes 524288 | tf_op jit(solution)/shard_map/all_to_all | solution.py:113
  230.1 252.7 %all-reduce = (f32[2,1]{0,1:T(1,128)S(1)}, f32[2,1]{0,1:T(1,128)S(1)}) all-reduce(f32[2,1]{0,1:T(1,128)S(1)} %bitcast.164, f32[2,1]{0,1:T(1,128)S(1)} %bitcast.165), channel_id=1, replica_groups=mesh['band'=128,'batch'=4] {'band'}, use_global_device_ids=true, to_apply=%region_13.15 | all-reduce | flops 4 | bytes 32 | tf_op jit(solution)/shard_map/psum | solution.py:131
  484.2 37.0 %all_to_all.34 = f32[128,2,2,128]{3,2,1,0:T(2,128)S(1)} all-to-all(f32[128,2,2,128]{3,2,1,0:T(2,128)S(1)} %copy.83), channel_id=1, replica_groups=mesh['band'=128,'batch'=4] {'band'}, dimensions={0} | all-to-all | bytes 524288 | tf_op jit(solution)/shard_map/all_to_all | solution.py:92
  521.3 0.7 gather_fusion.2
  522.0 8.4 %convolution_select_fusion = f32[128,2,128]{2,1,0:T(2,128)S(1)} fusion(f32[128,2,128]{2,1,0:T(2,128)S(1)} %gather_fusion.2, pred[128]{0:T(512)(128)(4,1)S(1)} %get-tuple-element.13, pred[128]{0:T(512)(128)(4,1)S(1)} %iota_compare_fusion.3, bf16[1,128,128,128]{3,2,1,0:T(8,128)(2,1)} %param.10), kind=kOutput, calls=%fused_computation.10 | convolution fusion | flops 50397184 | bytes 4456704 | tf_op jit(solution)/shard_map/tij,tkj->tki/dot_general | solution.py:96
  530.6 0.7 fusion.24
  (55 shorter events, 7.4 us)
Async XLA Ops:
  11.9 38.2 %all-to-all-start = ((s32[128,1,2]{2,1,0:T(1,128)}), s32[128,1,2]{2,1,0:T(1,128)S(1)}, u32[]{:S(2)}, u32[]{:S(2)}) async-start(s32[128,1,2]{2,1,0:T(1,128)} %bitcast.6), calls=%async_computation | async-start | bytes 131072 | tf_op jit(solution)/shard_map/all_to_all | solution.py:69
  32.5 71.6 %all-reduce.3.cloned.1.call-start = ((), (), s32[]{:S(2)}) async-start(), calls=%async_computation.6 | async-start | bytes 262144 | tf_op jit(solution)/shard_map/pmax | solution.py:67
  46.2 124.7 %copy-start.1 = (f32[2,256]{1,0:T(2,128)S(1)}, f32[2,256]{1,0:T(2,128)}, u32[]{:S(2)}) copy-start(f32[2,256]{1,0:T(2,128)} %param.16) | copy-start | bytes 6148
  46.2 124.7 %copy-start.2 = (f32[2,256]{1,0:T(2,128)S(1)}, f32[2,256]{1,0:T(2,128)}, u32[]{:S(2)}) copy-start(f32[2,256]{1,0:T(2,128)} %param.14) | copy-start | bytes 6148
  104.1 34.8 %all-to-all-start.1 = ((f32[128,2,128]{2,1,0:T(2,128)}), f32[128,2,128]{2,1,0:T(2,128)S(1)}, u32[]{:S(2)}, u32[]{:S(2)}) async-start(f32[128,2,128]{2,1,0:T(2,128)} %all-reduce.3.cloned.1.call-done), calls=%async_computation.1 | async-start | bytes 262144 | tf_op jit(solution)/shard_map/all_to_all | solution.py:70
  123.1 57.5 %copy-start.3 = (f32[512]{0:T(512)S(1)}, f32[512]{0:T(512)}, u32[]{:S(2)}) copy-start(f32[512]{0:T(512)} %param.15) | copy-start | bytes 6148
  133.3 77.1 %copy-start = (f32[2,512]{1,0:T(2,128)S(1)}, f32[2,512]{1,0:T(2,128)}, u32[]{:S(2)}) copy-start(f32[2,512]{1,0:T(2,128)} %param.17) | copy-start | bytes 12292
  138.9 31.8 %all-to-all-start.2 = ((f32[128,2,2,128]{3,1,2,0:T(2,128)}), f32[128,2,2,128]{3,1,2,0:T(2,128)S(1)}, u32[]{:S(2)}, u32[]{:S(2)}) async-start(f32[128,2,2,128]{3,1,2,0:T(2,128)} %copy.73), calls=%async_computation.2 | async-start | bytes 524288 | tf_op jit(solution)/shard_map/all_to_all | solution.py:113
  172.3 28.8 %all-to-all-start.3 = ((f32[128,2,2,128]{3,2,1,0:T(2,128)}), f32[128,2,2,128]{3,2,1,0:T(2,128)S(1)}, u32[]{:S(2)}, u32[]{:S(2)}) async-start(f32[128,2,2,128]{3,2,1,0:T(2,128)} %copy.75), calls=%async_computation.3 | async-start | bytes 524288 | tf_op jit(solution)/shard_map/all_to_all | solution.py:92
  221.8 261.0 %all-to-all-start.4 = ((f32[128,2,2,128]{3,1,2,0:T(2,128)}), f32[128,2,2,128]{3,1,2,0:T(2,128)S(1)}, u32[]{:S(2)}, u32[]{:S(2)}) async-start(f32[128,2,2,128]{3,1,2,0:T(2,128)} %copy.81), calls=%async_computation.4 | async-start | bytes 524288 | tf_op jit(solution)/shard_map/all_to_all | solution.py:113
Sparse Core Ops, SparseCore 0:
  49.5 54.5 all-reduce.2
where the time goes:
time: 540 us; the launch traced here: 538 us
  blocking collectives  299 us (55%)
  waiting for transfers between devices  99.5 us (18%)
  starting transfers between devices  67.2 us (12%)
  matrix products  28.9 us (5%)
  other arithmetic  21.6 us (4%)
  between operations  15 us (3%)
  local copies, waits for them, and re-layouts  7.16 us (1%)
    psum x1, blocking collectives, shards(): primal_step, dual_step = lax.psum((primal_step, dual_step), 'band')  253 us
    pmax x1, waiting for transfers between devices, shards(): col_send = lax.pmax(col_send, 'batch')  54.1 us
    all_to_all x1, blocking collectives, forward(): lax.all_to_all(replies, 'band', split_axis=0, concat_axis=0, tiled=True)  37 us
    all_to_all x1, starting transfers between devices, shards(): lax.all_to_all(requests, 'band', split_axis=0, concat_axis=0, tiled=True)  20.6 us
    all_to_all x1, waiting for transfers between devices, forward(): lax.all_to_all(replies, 'band', split_axis=0, concat_axis=0, tiled=True)  20.4 us
    all_to_all x2, waiting for transfers between devices, adjoint(): lax.all_to_all(outgoing.reshape(band_count, capacity, columns, tile_edge)...  20.2 us
    all_to_all x2, starting transfers between devices, adjoint(): lax.all_to_all(outgoing.reshape(band_count, capacity, columns, tile_edge)...  19.6 us
    all_to_all x1, starting transfers between devices, shards(): lax.all_to_all(col_send.reshape(band_count, capacity, tile_edge), 'band',...  18.7 us
  transfers between devices with their start and end apart: 6, of which 4 were waited for; matrix products, arithmetic and copies ran while one was open for 4% of the time, Pallas kernels for 0%

commit v1 on v0

v1 whole, which is shorter than its diff:
```python
import functools

import jax
import jax.numpy as jnp
from jax import lax
from jax.experimental import pallas as pl
from jax.experimental.pallas import tpu as pltpu
from jax.sharding import PartitionSpec as P

ROWBLK = 4
COLBLK = 2
PLANE = 8
UNROLL = 8

step_size = 0.0625
MESH = pl.DeviceIdType.MESH
F32 = jnp.float32
BF16 = jnp.bfloat16


def rows8():
    return lax.broadcasted_iota(jnp.int32, (8, 128), 0)


def split_parts(value):
    high = value.astype(BF16).astype(F32)
    return jnp.concatenate([high, value - high], axis=0).astype(BF16)


def place_of(owner, depth):
    return (owner % PLANE) * depth + owner // PLANE


def dual_rows(ref):
    return jnp.concatenate(
        [ref[k : k + 1, r * 128 : (r + 1) * 128] for k in range(2) for r in range(ROWBLK)], axis=0
    )


def bound_rows(ref):
    rows = [ref[0:1, r * 128 : (r + 1) * 128] for r in range(ROWBLK)]
    return jnp.concatenate(rows + rows, axis=0)


def fill_weights(weighted, table):
    row = rows8()
    for r in range(ROWBLK):
        first = jnp.broadcast_to(weighted[r : r + 1], (8, 128))
        second = jnp.broadcast_to(weighted[ROWBLK + r : ROWBLK + r + 1], (8, 128))
        for c in range(COLBLK):
            entry = jnp.where(row == 2 * c, first, jnp.where(row == 2 * c + 1, second, 0.0))
            table[r * COLBLK + c] = split_parts(entry)
    table[ROWBLK * COLBLK] = jnp.zeros((16, 128), BF16)


def forward_rows(tiles, tile_row, tile_col, count, gathered):
    ntile = tiles.shape[1]
    depth = gathered.shape[0] // (PLANE * COLBLK)
    row = rows8()

    def body(step, acc):
        for u in range(UNROLL):
            t = step * UNROLL + u
            r = jnp.where(t < count, tile_row[0, t], ROWBLK)
            col = tile_col[0, t]
            pair = gathered[place_of(col // COLBLK, depth) * COLBLK + col % COLBLK]
            value = jnp.where(
                row < ROWBLK,
                jnp.broadcast_to(pair[0:1], (8, 128)),
                jnp.broadcast_to(pair[1:2], (8, 128)),
            )
            value = jnp.where(row % ROWBLK == r, value, 0.0)
            acc = acc + lax.dot_general(
                split_parts(value),
                tiles[0, t],
                (((1,), (1,)), ((), ())),
                preferred_element_type=F32,
            )
        return acc

    acc = lax.fori_loop(0, ntile // UNROLL, body, jnp.zeros((16, 128), F32))
    return acc[0:8] + acc[8:16]


def scale_kernel(
    tiles, tile_row, tile_col, tile_count, y_start, outgoing, rscale, peaks, spread, table
):
    ntile = tiles.shape[1]
    depth = outgoing.shape[0] // PLANE
    count = tile_count[0]
    row = rows8()
    peaks[...] = jnp.zeros_like(peaks)

    def peak_body(step, carry):
        for u in range(UNROLL):
            t = step * UNROLL + u
            r = jnp.where(t < count, tile_row[0, t], ROWBLK)
            peaks[r] = jnp.maximum(peaks[r], jnp.abs(tiles[0, t]))
        return carry

    lax.fori_loop(0, ntile // UNROLL, peak_body, 0)
    rows = []
    for r in range(ROWBLK):
        peak = jnp.max(peaks[r].astype(F32), axis=1, keepdims=True)
        scale = jnp.broadcast_to(lax.rsqrt(peak), (128, 128))
        spread[r] = scale
        rows.append(jnp.transpose(scale)[0:1])
    spread[ROWBLK] = jnp.zeros((128, 128), F32)
    scales = jnp.concatenate(rows + rows, axis=0)
    rscale[...] = scales
    fill_weights(dual_rows(y_start) * scales, table)
    outgoing[...] = jnp.zeros_like(outgoing)

    def body(step, carry):
        for u in range(UNROLL):
            t = step * UNROLL + u
            r = jnp.where(t < count, tile_row[0, t], ROWBLK)
            col = tile_col[0, t]
            part = col % COLBLK
            place = place_of(col // COLBLK, depth)
            block = tiles[0, t]
            peak = jnp.max(jnp.abs(block.astype(F32)) * spread[r], axis=0, keepdims=True)
            peak = jnp.where(row == 4 + part, jnp.broadcast_to(peak, (8, 128)), 0.0)
            weights = table[jnp.minimum(r * COLBLK + part, ROWBLK * COLBLK)]
            product = jnp.dot(weights, block, preferred_element_type=F32)
            held = outgoing[place]
            outgoing[place] = jnp.where(
                row < 4, held + product[0:8] + product[8:16], jnp.maximum(held, peak)
            )
        return carry

    lax.fori_loop(0, ntile // UNROLL, body, 0)


def dual_kernel(
    tiles,
    tile_row,
    tile_col,
    tile_count,
    gathered,
    y_start,
    bound_vec,
    rscale,
    primal_step,
    outgoing,
    dual_out,
    table,
):
    ntile = tiles.shape[1]
    depth = outgoing.shape[0] // PLANE
    count = tile_count[0]
    row = rows8()
    scales = rscale[...]
    start = dual_rows(y_start)
    product = forward_rows(tiles, tile_row, tile_col, count, gathered) * scales
    dual = jnp.maximum(0.0, start + step_size * (bound_rows(bound_vec) * scales - product))
    dual_out[...] = dual
    move = (dual - start) ** 2
    first = jnp.sum(move[0:4], axis=0, keepdims=True)
    second = jnp.sum(move[4:8], axis=0, keepdims=True)
    steps = jnp.where(
        row == 6,
        jnp.broadcast_to(first, (8, 128)),
        jnp.where(row == 7, jnp.broadcast_to(second, (8, 128)), primal_step[...]),
    )
    fill_weights(dual * scales, table)
    outgoing[...] = jnp.broadcast_to(steps[None], outgoing.shape)

    def body(step, carry):
        for u in range(UNROLL):
            t = step * UNROLL + u
            r = jnp.where(t < count, tile_row[0, t], ROWBLK)
            col = tile_col[0, t]
            place = place_of(col // COLBLK, depth)
            weights = table[jnp.minimum(r * COLBLK + col % COLBLK, ROWBLK * COLBLK)]
            product = jnp.dot(weights, tiles[0, t], preferred_element_type=F32)
            outgoing[place] = outgoing[place] + product[0:8] + product[8:16]
        return carry

    lax.fori_loop(0, ntile // UNROLL, body, 0)


def final_kernel(
    tiles, tile_row, tile_col, tile_count, gathered, bound_vec, rscale, dual_in, step_in, y_out
):
    scales = rscale[...]
    product = forward_rows(tiles, tile_row, tile_col, tile_count[0], gathered) * scales
    dual = jnp.maximum(
        0.0, dual_in[...] + step_in[...] * (bound_rows(bound_vec) * scales - product)
    )
    for k in range(2):
        for r in range(ROWBLK):
            y_out[k : k + 1, r * 128 : (r + 1) * 128] = dual[k * ROWBLK + r : k * ROWBLK + r + 1]


def primal_rows(ref):
    return jnp.concatenate(
        [ref[k : k + 1, c * 128 : (c + 1) * 128] for c in range(COLBLK) for k in range(2)], axis=0
    )


def exchange(depth, combine, update, outgoing, gathered, scratch):
    (in_plane, reduced, in_line, sem_a, sem_b, sem_c, sem_d) = scratch
    me = lax.axis_index("band")
    z = me // PLANE
    p = me % PLANE
    plane_peers = [(p + d) % PLANE for d in range(1, PLANE)]
    line_peers = [(z + d) % depth for d in range(1, depth)]

    barrier = pltpu.get_barrier_semaphore()
    for q in plane_peers:
        pl.semaphore_signal(
            barrier, inc=1, device_id={"band": z * PLANE + q}, device_id_type=MESH
        )
    for q in line_peers:
        pl.semaphore_signal(
            barrier, inc=1, device_id={"band": q * PLANE + p}, device_id_type=MESH
        )
    pl.semaphore_wait(barrier, len(plane_peers) + len(line_peers))

    def send(src, dst, sems, slot, band):
        copy = pltpu.make_async_remote_copy(
            src_ref=src,
            dst_ref=dst,
            send_sem=sems.at[0, slot],
            recv_sem=sems.at[1, slot],
            device_id={"band": band},
            device_id_type=MESH,
        )
        copy.start()
        return copy

    first = [
        send(
            outgoing.at[pl.ds(q * depth, depth)], in_plane.at[i], sem_a, i, z * PLANE + q
        )
        for i, q in enumerate(plane_peers)
    ]
    total = outgoing[pl.ds(p * depth, depth)]
    for i, copy in enumerate(first):
        copy.wait_recv()
        total = combine(total, in_plane[i])
    reduced[...] = total
    second = [
        send(reduced.at[q], in_line.at[i], sem_b, i, q * PLANE + p)
        for i, q in enumerate(line_peers)
    ]
    mine = reduced[z]
    for i, copy in enumerate(second):
        copy.wait_recv()
        mine = combine(mine, in_line[i])
    block = update(mine)
    at = (p * depth + z) * COLBLK
    for c in range(COLBLK):
        gathered[at + c] = block[2 * c : 2 * c + 2]
    third = [
        send(
            gathered.at[pl.ds(at, COLBLK)], gathered.at[pl.ds(at, COLBLK)], sem_c, i, q * PLANE + p
        )
        for i, q in enumerate(line_peers)
    ]
    for copy in third:
        copy.wait_recv()
    span = depth * COLBLK
    fourth = [
        send(
            gathered.at[pl.ds(p * span, span)],
            gathered.at[pl.ds(p * span, span)],
            sem_d,
            i,
            z * PLANE + q,
        )
        for i, q in enumerate(plane_peers)
    ]
    for copy in fourth:
        copy.wait_recv()
    for copy in first + second + third + fourth:
        copy.wait_send()


def primal_kernel(depth, outgoing, cost, x_start, gathered, primal_out, cscale, primal_step, *scratch):
    def combine(a, b):
        row = lax.broadcasted_iota(jnp.int32, a.shape, a.ndim - 2)
        return jnp.where(row < 4, a + b, jnp.maximum(a, b))

    def update(mine):
        row = lax.broadcasted_iota(jnp.int32, (4, 128), 0)
        scales = lax.rsqrt(
            jnp.where(
                row < 2,
                jnp.broadcast_to(mine[4:5], (4, 128)),
                jnp.broadcast_to(mine[5:6], (4, 128)),
            )
        )
        start = primal_rows(x_start)
        primal = jnp.maximum(
            0.0, start - step_size * (primal_rows(cost) * scales - mine[0:4] * scales)
        )
        primal_out[...] = primal
        cscale[...] = scales
        move = (primal - start) ** 2
        move = move[0:2] + move[2:4]
        zeros = jnp.zeros((4, 128), F32)
        primal_step[...] = jnp.concatenate([zeros, move, zeros[0:2]], axis=0)
        return (2.0 * primal - start) * scales

    exchange(depth, combine, update, outgoing, gathered, scratch)


def second_kernel(depth, outgoing, cost, primal_in, cscale, gathered, x_out, dual_step, *scratch):
    def update(mine):
        row = lax.broadcasted_iota(jnp.int32, (4, 128), 0)
        sums = jnp.sum(mine[4:8], axis=1, keepdims=True) + 1e-06
        omega = jnp.sqrt(sums[2:4] / sums[0:2])
        omega = jnp.broadcast_to(omega, (2, 128))
        wide = jnp.concatenate([omega, omega], axis=0)
        dual_step[...] = jnp.concatenate(
            [
                jnp.broadcast_to(step_size * omega[0:1], (4, 128)),
                jnp.broadcast_to(step_size * omega[1:2], (4, 128)),
            ],
            axis=0,
        )
        scales = cscale[...]
        before = primal_in[...]
        primal = jnp.maximum(
            0.0, before - (step_size / wide) * (primal_rows(cost) * scales - mine[0:4] * scales)
        )
        for c in range(COLBLK):
            x_out[:, c * 128 : (c + 1) * 128] = primal[2 * c : 2 * c + 2]
        return (2.0 * primal - before) * scales

    exchange(depth, lambda a, b: a + b, update, outgoing, gathered, scratch)


VMEM = pl.BlockSpec(memory_space=pltpu.VMEM)
SMEM = pl.BlockSpec(memory_space=pltpu.SMEM)
LIMIT = 40 << 20


def shards(tiles, tile_row, tile_col, tile_count, cost, bound_vec, x_start, y_start):
    bands = lax.axis_size("band")
    depth = bands // PLANE
    bound_vec = bound_vec.reshape(1, -1)

    def shape(*dims):
        return jax.ShapeDtypeStruct(dims, F32)

    index = (tile_row, tile_col, tile_count)
    local = [VMEM, SMEM, SMEM, SMEM]
    params = pltpu.CompilerParams(vmem_limit_bytes=LIMIT)
    table = pltpu.VMEM((ROWBLK * COLBLK + 1, 16, 128), BF16)

    def comm(kernel, ident, out_shape, nin):
        return pl.pallas_call(
            functools.partial(kernel, depth),
            out_shape=out_shape,
            in_specs=[VMEM] * nin,
            out_specs=[VMEM] * len(out_shape),
            scratch_shapes=[
                pltpu.VMEM((PLANE - 1, depth, 8, 128), F32),
                pltpu.VMEM((depth, 8, 128), F32),
                pltpu.VMEM((depth - 1, 8, 128), F32),
                pltpu.SemaphoreType.DMA((2, PLANE - 1)),
                pltpu.SemaphoreType.DMA((2, depth - 1)),
                pltpu.SemaphoreType.DMA((2, depth - 1)),
                pltpu.SemaphoreType.DMA((2, PLANE - 1)),
            ],
            compiler_params=pltpu.CompilerParams(
                collective_id=ident, has_side_effects=True, vmem_limit_bytes=LIMIT
            ),
        )

    outgoing, rscale = pl.pallas_call(
        scale_kernel,
        out_shape=(shape(bands, 8, 128), shape(8, 128)),
        in_specs=local + [VMEM],
        out_specs=(VMEM, VMEM),
        scratch_shapes=[
            pltpu.VMEM((ROWBLK + 1, 128, 128), BF16),
            pltpu.VMEM((ROWBLK + 1, 128, 128), F32),
            table,
        ],
        compiler_params=params,
    )(tiles, *index, y_start)
    gathered, primal, cscale, primal_step = comm(
        primal_kernel,
        0,
        (shape(bands * COLBLK, 2, 128), shape(4, 128), shape(4, 128), shape(8, 128)),
        3,
    )(outgoing, cost, x_start)
    outgoing, dual = pl.pallas_call(
        dual_kernel,
        out_shape=(shape(bands, 8, 128), shape(8, 128)),
        in_specs=local + [VMEM] * 5,
        out_specs=(VMEM, VMEM),
        scratch_shapes=[table],
        compiler_params=params,
    )(tiles, *index, gathered, y_start, bound_vec, rscale, primal_step)
    gathered, x_out, dual_step = comm(
        second_kernel, 1, (shape(bands * COLBLK, 2, 128), shape(2, COLBLK * 128), shape(8, 128)), 4
    )(outgoing, cost, primal, cscale)
    y_out = pl.pallas_call(
        final_kernel,
        out_shape=shape(2, ROWBLK * 128),
        in_specs=local + [VMEM] * 5,
        out_specs=VMEM,
        compiler_params=params,
    )(tiles, *index, gathered, bound_vec, rscale, dual, dual_step)
    return (x_out, y_out)


def solution(mesh):
    return jax.shard_map(
        shards,
        mesh=mesh,
        in_specs=(
            P("band", None, None, None),
            P("band", None),
            P("band", None),
            P("band"),
            P("batch", "band"),
            P("band"),
            P("batch", "band"),
            P("batch", "band"),
        ),
        out_specs=(P("batch", "band"), P("batch", "band")),
        check_vma=False,
    )
```

time: 540 us -> 103 us (0.19)
  blocking collectives: 299 us -> 0 us
  waiting for transfers between devices: 99.5 us -> 0 us
  Pallas kernels: 0 us -> 96.1 us
  starting transfers between devices: 67.2 us -> 0 us
  matrix products: 28.9 us -> 0 us
  other arithmetic: 21.6 us -> 0 us
  between operations: 15 us -> 1.36 us
    psum x1 -> x0, blocking collectives: 253 us -> none  [shards(): primal_step, dual_step = lax.psum((primal_step, dual_step), 'band')]
    pallas_call x0 -> x5, Pallas kernels: none -> 96.1 us  [the longest x1 46.3 us: shards(): comm(primal_kernel, 0, (shape(bands * COLBLK, 2, 128), shape(4, 128), sha...]
    all_to_all x5 -> x0, starting transfers between devices: 67.2 us -> none  [the longest x1 20.6 us: shards(): lax.all_to_all(requests, 'band', split_axis=0, concat_axis=0, tiled=True)]
    pmax x1 -> x0, waiting for transfers between devices: 54.1 us -> none  [shards(): col_send = lax.pmax(col_send, 'batch')]
    all_to_all x5 -> x0, waiting for transfers between devices: 45.4 us -> none  [the longest x1 20.4 us: forward(): lax.all_to_all(replies, 'band', split_axis=0, concat_axis=0, tiled=True)]
    all_to_all x1 -> x0, blocking collectives: 37 us -> none  [forward(): lax.all_to_all(replies, 'band', split_axis=0, concat_axis=0, tiled=True)]
    dot_general x12 -> x0, matrix products: 28.9 us -> none  [the longest x2 16.8 us: forward(): product = jnp.einsum('tij,tkj->tki', widened, picked, precision=high)]
    scatter-add x2 -> x0, other arithmetic: 9.99 us -> none  [adjoint(): outgoing = jnp.zeros((overflow, columns, tile_edge), jnp.float32).at[slot...]
  transfers between devices with their start and end apart: 6 -> 0, of which waited for: 4 -> 0; matrix products, arithmetic and copies ran while one was open for 4% -> 0% of each run, Pallas kernels for 0% -> 0%
where the time goes in v1:
time: 103 us; the launch traced here: 102 us
  Pallas kernels  96.1 us (93%)
  local copies, waits for them, and re-layouts  4.77 us (5%)
  between operations  1.36 us (1%)
    pallas_call x1, Pallas kernels, shards(): comm(primal_kernel, 0, (shape(bands * COLBLK, 2, 128), shape(4, 128), sha...  46.3 us
    pallas_call x1, Pallas kernels, shards(): comm(second_kernel, 1, (shape(bands * COLBLK, 2, 128), shape(2, COLBLK *...  31.7 us
    pallas_call x1, Pallas kernels, shards(): pl.pallas_call(dual_kernel, out_shape=(shape(bands, 8, 128), shape(8, 128...  7.71 us
    pallas_call x1, Pallas kernels, shards(): pl.pallas_call(final_kernel, out_shape=shape(2, ROWBLK * 128), in_specs=l...  5.22 us
    pallas_call x1, Pallas kernels, shards(): pl.pallas_call(scale_kernel, out_shape=(shape(bands, 8, 128), shape(8, 12...  5.18 us
    unnamed x17, local copies, waits for them, and re-layouts  4.77 us

profile of v1, /device:TPU:1, one launch (start us, length us, event | category | flops | bytes accessed | tf_op | source)
XLA Modules:
  0.0 102.3 jit_solution(15986510342657576938)
XLA Ops:
  0.6 0.0 copy-start.3
  1.3 0.0 copy-start
  1.3 2.2 %copy-done = bf16[1,128,128,128]{3,2,1,0:T(8,128)(2,1)S(1)} copy-done((bf16[1,128,128,128]{3,2,1,0:T(8,128)(2,1)S(1)}, bf16[1,128,128,128]{3,2,1,0:T(8,128)(2,1)}, u32[]{:S(2)}) %copy-start) | copy-done | bytes 4194328
  3.5 0.0 copy-start.2
  3.5 0.7 copy-done.2
  4.2 0.0 copy-start.5
  4.2 0.7 copy-done.5
  4.8 0.0 copy-start.6
  4.8 0.7 copy-done.6
  5.5 0.0 copy-start.4
  5.5 0.0 copy-start.7
  5.5 0.0 copy-start.1
  5.5 5.2 %shard_map.95 = (f32[128,8,128]{2,1,0:T(8,128)S(1)}, f32[8,128]{1,0:T(8,128)S(1)}) custom-call(bf16[1,128,128,128]{3,2,1,0:T(8,128)(2,1)S(1)} %copy-done, s32[1,128]{1,0:T(1,128)S(1)} %copy-done.5, s32[1,128]{1,0:T(1,128)S(1)} %copy-done.6, s32[1]{0:T(128)S(6)} %copy.11.tile_count, f32[2,512]{1,0:T(2,128)S(1)} %copy-done.2), custom_call_target="tpu_custom_call" | custom-call | tf_op jit(solution)/shard_map/pallas_call | solution.py:374
  10.7 0.0 copy-done.4
  10.7 0.0 copy-done.7
  10.7 46.3 %shard_map.96 = (f32[256,2,128]{2,1,0:T(2,128)S(1)}, f32[4,128]{1,0:T(4,128)S(1)}, f32[4,128]{1,0:T(4,128)S(1)}, f32[8,128]{1,0:T(8,128)S(1)}) custom-call(f32[128,8,128]{2,1,0:T(8,128)S(1)} %get-tuple-element.13.outgoing, f32[2,256]{1,0:T(2,128)S(1)} %copy-done.4, f32[2,256]{1,0:T(2,128)S(1)} %copy-done.7), custom_call_target="tpu_custom_call" | custom-call | tf_op jit(solution)/shard_map/pallas_call | solution.py:386
  57.0 0.0 copy-done.3
  57.0 0.0 copy-done.1
  57.0 7.7 %shard_map.97 = (f32[128,8,128]{2,1,0:T(8,128)S(1)}, f32[8,128]{1,0:T(8,128)S(1)}) custom-call(bf16[1,128,128,128]{3,2,1,0:T(8,128)(2,1)S(1)} %copy-done.1, s32[1,128]{1,0:T(1,128)S(1)} %copy-done.5, s32[1,128]{1,0:T(1,128)S(1)} %copy-done.6, s32[1]{0:T(128)S(6)} %copy.11.tile_count, f32[256,2,128]{2,1,0:T(2,128)S(1)} %get-tuple-element.14.gathered, ...), custom_call_target="tpu_custom_call" | custom-call | tf_op jit(solution)/shard_map/pallas_call | solution.py:392
  64.7 31.7 %shard_map.98 = (f32[256,2,128]{2,1,0:T(2,128)S(1)}, f32[2,256]{1,0:T(2,128)S(1)}, f32[8,128]{1,0:T(8,128)S(1)}) custom-call(f32[128,8,128]{2,1,0:T(8,128)S(1)} %get-tuple-element.17.outgoing, f32[2,256]{1,0:T(2,128)S(1)} %copy-done.4, f32[4,128]{1,0:T(4,128)S(1)} %get-tuple-element.18.primal_in, f32[4,128]{1,0:T(4,128)S(1)} %get-tuple-element.19.cscale), custom_call_target="tpu_custom_call" | custom-call | tf_op jit(solution)/shard_map/pallas_call | solution.py:400
  96.5 5.2 %shard_map.99 = f32[2,512]{1,0:T(2,128)} custom-call(bf16[1,128,128,128]{3,2,1,0:T(8,128)(2,1)S(1)} %copy-done.1, s32[1,128]{1,0:T(1,128)S(1)} %copy-done.5, s32[1,128]{1,0:T(1,128)S(1)} %copy-done.6, s32[1]{0:T(128)S(6)} %copy.11.tile_count, f32[256,2,128]{2,1,0:T(2,128)S(1)} %get-tuple-element.21.gathered, f32[1,512]{1,0:T(1,128)S(1)} %bitcast.2, ...), custom_call_target="tpu_custom_call" | custom-call | tf_op jit(solution)/shard_map/pallas_call | solution.py:403
  101.7 0.6 copy.12
Async XLA Ops:
  0.6 56.4 %copy-start.3 = (f32[512]{0:T(512)S(1)}, f32[512]{0:T(512)}, u32[]{:S(2)}) copy-start(f32[512]{0:T(512)} %param.13) | copy-start | bytes 6148
  1.3 2.2 %copy-start = (bf16[1,128,128,128]{3,2,1,0:T(8,128)(2,1)S(1)}, bf16[1,128,128,128]{3,2,1,0:T(8,128)(2,1)}, u32[]{:S(2)}) copy-start(bf16[1,128,128,128]{3,2,1,0:T(8,128)(2,1)} %tiles.5) | copy-start | bytes 12582916
  3.5 0.7 copy-start.2
  4.2 0.7 copy-start.5
  4.8 0.7 copy-start.6
  5.5 5.2 %copy-start.4 = (f32[2,256]{1,0:T(2,128)S(1)}, f32[2,256]{1,0:T(2,128)}, u32[]{:S(2)}) copy-start(f32[2,256]{1,0:T(2,128)} %cost.3) | copy-start | bytes 6148
  5.5 5.2 %copy-start.7 = (f32[2,256]{1,0:T(2,128)S(1)}, f32[2,256]{1,0:T(2,128)}, u32[]{:S(2)}) copy-start(f32[2,256]{1,0:T(2,128)} %x_start.1) | copy-start | bytes 6148
  5.5 51.5 %copy-start.1 = (bf16[1,128,128,128]{3,2,1,0:T(8,128)(2,1)S(1)}, bf16[1,128,128,128]{3,2,1,0:T(8,128)(2,1)}, u32[]{:S(2)}) copy-start(bf16[1,128,128,128]{3,2,1,0:T(8,128)(2,1)} %tiles.5) | copy-start | bytes 12582916

commit v2 on v0

v2 whole, which is shorter than its diff:
```python
import jax
import jax.numpy as jnp
from jax import lax
from jax.experimental import pallas as pl
from jax.experimental.pallas import tpu as pltpu
from jax.sharding import PartitionSpec as P

ROWBLK = 4
COLBLK = 2
PLANE = 8
UNROLL = 8
PIECE = 16

step_size = 0.0625
MESH = pl.DeviceIdType.MESH
F32 = jnp.float32
BF16 = jnp.bfloat16


def rows8():
    return lax.broadcasted_iota(jnp.int32, (8, 128), 0)


def split_parts(value):
    high = value.astype(BF16).astype(F32)
    return jnp.concatenate([high, value - high], axis=0).astype(BF16)


def slot_of(offset, depth):
    if isinstance(offset, int):
        return max(2 * offset - 1, 0) if offset <= depth // 2 else 2 * (depth - offset)
    ahead = jnp.maximum(2 * offset - 1, 0)
    return jnp.where(offset <= depth // 2, ahead, 2 * (depth - offset))


def offset_of(slot, depth):
    return (slot + 1) // 2 if slot % 2 == 1 else (depth - slot // 2) % depth


def dual_rows(ref):
    return jnp.concatenate(
        [ref[k : k + 1, r * 128 : (r + 1) * 128] for k in range(2) for r in range(ROWBLK)], axis=0
    )


def bound_rows(ref):
    rows = [ref[0:1, r * 128 : (r + 1) * 128] for r in range(ROWBLK)]
    return jnp.concatenate(rows + rows, axis=0)


def primal_rows(ref):
    return jnp.concatenate(
        [ref[k : k + 1, c * 128 : (c + 1) * 128] for c in range(COLBLK) for k in range(2)], axis=0
    )


def fill_weights(weighted, table):
    row = rows8()
    for r in range(ROWBLK):
        first = jnp.broadcast_to(weighted[r : r + 1], (8, 128))
        second = jnp.broadcast_to(weighted[ROWBLK + r : ROWBLK + r + 1], (8, 128))
        for c in range(COLBLK):
            entry = jnp.where(row == 2 * c, first, jnp.where(row == 2 * c + 1, second, 0.0))
            table[r * COLBLK + c] = split_parts(entry)
    table[ROWBLK * COLBLK] = jnp.zeros((16, 128), BF16)


def kernel(
    tiles_in,
    tile_row,
    tile_col,
    tile_count,
    first_of,
    second_of,
    cost,
    bound_vec,
    x_start,
    y_start,
    x_out,
    y_out,
    tiles,
    flipped,
    spread,
    table,
    parts,
    wide_out,
    wide_in,
    slim_out,
    slim_in,
    steps_out,
    steps_in,
    reduced,
    line_in,
    gathered,
    tile_sem,
    plane_sem,
    steps_sem,
    line_sem,
    back_line_sem,
    back_plane_sem,
):
    ntile = tiles.shape[0]
    depth = reduced.shape[1]
    half = depth // 2
    chunks = ((0, half), (half, depth))
    me = lax.axis_index("band")
    z = me // PLANE
    p = me % PLANE
    plane_peer = {d: z * PLANE + (p + d) % PLANE for d in range(1, PLANE)}
    line_peer = {d: ((z + d) % depth) * PLANE + p for d in range(1, depth)}
    count = tile_count[0]
    row = rows8()
    started = []

    barrier = pltpu.get_barrier_semaphore()
    for band in list(plane_peer.values()) + list(line_peer.values()):
        pl.semaphore_signal(barrier, inc=1, device_id={"band": band}, device_id_type=MESH)

    def piece_copy(i):
        at = pl.ds(i * PIECE, PIECE)
        return pltpu.make_async_copy(tiles_in.at[0, at], tiles.at[at], tile_sem.at[i])

    for i in range(ntile // PIECE):
        piece_copy(i).start()

    def send(src, dst, send_sem, recv_sem, band):
        copy = pltpu.make_async_remote_copy(
            src_ref=src,
            dst_ref=dst,
            send_sem=send_sem,
            recv_sem=recv_sem,
            device_id={"band": band},
            device_id_type=MESH,
        )
        copy.start()
        started.append(copy)
        return copy

    def live_row(t):
        return jnp.where(t < count, tile_row[0, t], ROWBLK)

    def peak_piece(i, peaks):
        piece_copy(i).wait()

        def peak_body(step, peaks):
            peaks = list(peaks)
            for u in range(UNROLL):
                t = i * PIECE + step * UNROLL + u
                r = live_row(t)
                size = jnp.abs(tiles[t])
                for k in range(ROWBLK):
                    peaks[k] = jnp.maximum(peaks[k], jnp.where(r == k, size, jnp.zeros_like(size)))
            return tuple(peaks)

        return lax.fori_loop(0, PIECE // UNROLL, peak_body, peaks)

    peaks = lax.fori_loop(
        0, ntile // PIECE, peak_piece, (jnp.zeros((128, 128), BF16),) * ROWBLK
    )
    lines = []
    for r in range(ROWBLK):
        peak = jnp.max(peaks[r].astype(F32), axis=1, keepdims=True)
        scale = jnp.broadcast_to(lax.rsqrt(peak), (128, 128))
        spread[r] = scale
        lines.append(jnp.transpose(scale)[0:1])
    spread[ROWBLK] = jnp.zeros((128, 128), F32)
    rscale = jnp.concatenate(lines + lines, axis=0)
    start = dual_rows(y_start)
    sbound = bound_rows(bound_vec) * rscale
    fill_weights(start * rscale, table)
    parts[ntile] = jnp.zeros((8, 128), F32)

    def weights_of(t, r):
        return table[jnp.minimum(r * COLBLK + tile_col[0, t] % COLBLK, ROWBLK * COLBLK)]

    def scale_body(step, carry):
        for u in range(UNROLL):
            t = step * UNROLL + u
            r = live_row(t)
            block = tiles[t]
            peak = jnp.max(jnp.abs(block.astype(F32)) * spread[r], axis=0, keepdims=True)
            peak = jnp.broadcast_to(peak, (8, 128))
            product = jnp.dot(weights_of(t, r), block, preferred_element_type=F32)
            parts[t] = jnp.where(
                row < 4,
                product[0:8] + product[8:16],
                jnp.where(row == 4 + tile_col[0, t] % COLBLK, peak, 0.0),
            )
        return carry

    lax.fori_loop(0, ntile // UNROLL, scale_body, 0)

    def adjoint_body(step, carry):
        for u in range(UNROLL):
            t = step * UNROLL + u
            product = jnp.dot(weights_of(t, live_row(t)), tiles[t], preferred_element_type=F32)
            parts[t] = product[0:8] + product[8:16]
        return carry

    def place_parts(store):
        def body(slot, carry):
            odd = slot % 2
            offset = odd * ((slot + 1) // 2) + (1 - odd) * ((depth - slot // 2) % depth)
            for d in range(PLANE):
                owner = ((z + offset) % depth) * PLANE + (p + d) % PLANE
                store(d, slot, parts[first_of[owner]], parts[second_of[owner]])
            return carry

        lax.fori_loop(0, depth, body, 0)

    def store_wide(d, slot, a, b):
        wide_out[d, slot] = jnp.where(row < 4, a + b, jnp.maximum(a, b))

    def store_slim(d, slot, a, b):
        slim_out[d, slot] = (a + b)[0:4]

    def reduce_scatter(turn, out, into, combine, steps=None):
        plane = {}
        if steps is not None:
            steps_out[...] = steps
            for d in range(1, PLANE):
                plane[d] = send(
                    steps_out,
                    steps_in.at[d - 1],
                    steps_sem.at[0, d - 1],
                    steps_sem.at[1, d - 1],
                    plane_peer[d],
                )
        for n, (lo, hi) in reversed(tuple(enumerate(chunks))):
            for d in range(1, PLANE):
                plane[d, n] = send(
                    out.at[d, pl.ds(lo, hi - lo)],
                    into.at[d - 1, pl.ds(lo, hi - lo)],
                    plane_sem.at[turn, 0, n, d - 1],
                    plane_sem.at[turn, 1, n, d - 1],
                    plane_peer[d],
                )
        if steps is not None:
            for d in range(1, PLANE):
                plane[d].wait_recv()
                steps = steps + steps_in[d - 1]
        line = {}
        for n, (lo, hi) in reversed(tuple(enumerate(chunks))):
            total = out[0, lo:hi]
            for d in range(1, PLANE):
                plane[d, n].wait_recv()
                total = combine(total, into[d - 1, lo:hi])
            if steps is None:
                reduced[turn, lo:hi] = total
            else:
                reduced[turn, lo:hi, 0:4] = total
                reduced[turn, lo:hi, 4:8] = jnp.broadcast_to(steps[None], (hi - lo, 4, 128))
            for slot in range(hi - 1, max(lo, 1) - 1, -1):
                back = slot_of((depth - offset_of(slot, depth)) % depth, depth)
                line[back] = send(
                    reduced.at[turn, slot],
                    line_in.at[turn, back],
                    line_sem.at[turn, 0, slot],
                    line_sem.at[turn, 1, back],
                    line_peer[offset_of(slot, depth)],
                )
        return line

    def collect(turn, line, combine):
        mine = reduced[turn, 0]
        for slot in range(1, depth):
            line[slot].wait_recv()
        for slot in range(1, depth):
            mine = combine(mine, line_in[turn, slot])
        return mine

    def all_gather(turn, block):
        for c in range(COLBLK):
            gathered[turn, 0, 0, c] = block[2 * c : 2 * c + 2]
        line = {}
        for slot in range(depth - 1, 0, -1):
            back = slot_of((depth - offset_of(slot, depth)) % depth, depth)
            line[slot] = send(
                gathered.at[turn, 0, 0],
                gathered.at[turn, 0, back],
                back_line_sem.at[turn, 0, slot],
                back_line_sem.at[turn, 1, back],
                line_peer[offset_of(slot, depth)],
            )
        plane = []
        for n, (lo, hi) in enumerate(chunks):
            for slot in range(max(lo, 1), hi):
                pltpu.make_async_remote_copy(
                    src_ref=gathered.at[turn, 0, 0],
                    dst_ref=gathered.at[turn, 0, slot],
                    send_sem=back_line_sem.at[turn, 0, slot],
                    recv_sem=back_line_sem.at[turn, 1, slot],
                    device_id={"band": line_peer[offset_of(slot, depth)]},
                    device_id_type=MESH,
                ).wait_recv()
            for d in range(1, PLANE):
                plane.append(
                    send(
                        gathered.at[turn, 0, pl.ds(lo, hi - lo)],
                        gathered.at[turn, PLANE - d, pl.ds(lo, hi - lo)],
                        back_plane_sem.at[turn, 0, n, d - 1],
                        back_plane_sem.at[turn, 1, n, d - 1],
                        plane_peer[d],
                    )
                )
        for copy in plane:
            copy.wait_recv()

    def forward(turn):
        def body(step, acc):
            for u in range(UNROLL):
                t = step * UNROLL + u
                r = live_row(t)
                col = tile_col[0, t]
                owner = col // COLBLK
                d = (owner % PLANE + PLANE - p) % PLANE
                slot = slot_of((owner // PLANE + depth - z) % depth, depth)
                pair = gathered[turn, d, slot, col % COLBLK]
                value = jnp.where(
                    row < ROWBLK,
                    jnp.broadcast_to(pair[0:1], (8, 128)),
                    jnp.broadcast_to(pair[1:2], (8, 128)),
                )
                value = jnp.where(row % ROWBLK == r, value, 0.0)
                acc = acc + jnp.dot(split_parts(value), flipped[t], preferred_element_type=F32)
            return acc

        acc = lax.fori_loop(0, ntile // UNROLL, body, jnp.zeros((16, 128), F32))
        return (acc[0:8] + acc[8:16]) * rscale

    def join(a, b):
        top = lax.broadcasted_iota(jnp.int32, a.shape, a.ndim - 2) < 4
        return jnp.where(top, a + b, jnp.maximum(a, b))

    def add(a, b):
        return a + b

    place_parts(store_wide)
    pl.semaphore_wait(barrier, PLANE - 1 + depth - 1)
    line = reduce_scatter(0, wide_out, wide_in, join)

    def flip_body(step, carry):
        for u in range(UNROLL):
            t = step * UNROLL + u
            flipped[t] = jnp.transpose(tiles[t])
        return carry

    lax.fori_loop(0, ntile // UNROLL, flip_body, 0)
    mine = collect(0, line, join)

    row4 = lax.broadcasted_iota(jnp.int32, (4, 128), 0)
    cscale = lax.rsqrt(
        jnp.where(
            row4 < 2,
            jnp.broadcast_to(mine[4:5], (4, 128)),
            jnp.broadcast_to(mine[5:6], (4, 128)),
        )
    )
    before = primal_rows(x_start)
    scost = primal_rows(cost) * cscale
    primal = jnp.maximum(0.0, before - step_size * (scost - mine[0:4] * cscale))
    all_gather(0, (2.0 * primal - before) * cscale)
    move = (primal - before) ** 2
    dual = jnp.maximum(0.0, start + step_size * (sbound - forward(0)))
    fill_weights(dual * rscale, table)
    turn = (dual - start) ** 2
    steps = jnp.concatenate(
        [
            move[0:2] + move[2:4],
            jnp.sum(turn[0:4], axis=0, keepdims=True),
            jnp.sum(turn[4:8], axis=0, keepdims=True),
        ],
        axis=0,
    )

    lax.fori_loop(0, ntile // UNROLL, adjoint_body, 0)
    place_parts(store_slim)
    mine = collect(1, reduce_scatter(1, slim_out, slim_in, add, steps), add)
    sums = jnp.sum(mine[4:8], axis=1, keepdims=True) + 1e-06
    omega = jnp.broadcast_to(jnp.sqrt(sums[2:4] / sums[0:2]), (2, 128))
    wide = jnp.concatenate([omega, omega], axis=0)
    after = jnp.maximum(0.0, primal - (step_size / wide) * (scost - mine[0:4] * cscale))
    all_gather(1, (2.0 * after - primal) * cscale)
    for c in range(COLBLK):
        x_out[:, c * 128 : (c + 1) * 128] = after[2 * c : 2 * c + 2]
    pace = jnp.concatenate(
        [
            jnp.broadcast_to(step_size * omega[0:1], (4, 128)),
            jnp.broadcast_to(step_size * omega[1:2], (4, 128)),
        ],
        axis=0,
    )
    last = jnp.maximum(0.0, dual + pace * (sbound - forward(1)))
    for k in range(2):
        for r in range(ROWBLK):
            y_out[k : k + 1, r * 128 : (r + 1) * 128] = last[k * ROWBLK + r : k * ROWBLK + r + 1]
    for copy in started:
        copy.wait_send()


VMEM = pl.BlockSpec(memory_space=pltpu.VMEM)
SMEM = pl.BlockSpec(memory_space=pltpu.SMEM)


def shards(tiles, tile_row, tile_col, tile_count, cost, bound_vec, x_start, y_start):
    ntile = tiles.shape[1]
    bands = lax.axis_size("band")
    depth = bands // PLANE
    index = jnp.arange(ntile, dtype=jnp.int32)[None, :]
    match = (tile_col // COLBLK == jnp.arange(bands, dtype=jnp.int32)[:, None]) & (
        index < tile_count[0]
    )
    first_of = jnp.min(jnp.where(match, index, ntile), axis=1)
    second_of = jnp.max(jnp.where(match, index, -1), axis=1)
    second_of = jnp.where(second_of > first_of, second_of, ntile)

    dma = pltpu.SemaphoreType.DMA
    return pl.pallas_call(
        kernel,
        out_shape=(
            jax.ShapeDtypeStruct((2, COLBLK * 128), F32),
            jax.ShapeDtypeStruct((2, ROWBLK * 128), F32),
        ),
        in_specs=[pl.BlockSpec(memory_space=pl.ANY)] + [SMEM] * 5 + [VMEM] * 4,
        out_specs=(VMEM, VMEM),
        scratch_shapes=[
            pltpu.VMEM((ntile, 128, 128), BF16),
            pltpu.VMEM((ntile, 128, 128), BF16),
            pltpu.VMEM((ROWBLK + 1, 128, 128), F32),
            pltpu.VMEM((ROWBLK * COLBLK + 1, 16, 128), BF16),
            pltpu.VMEM((ntile + 1, 8, 128), F32),
            pltpu.VMEM((PLANE, depth, 8, 128), F32),
            pltpu.VMEM((PLANE - 1, depth, 8, 128), F32),
            pltpu.VMEM((PLANE, depth, 4, 128), F32),
            pltpu.VMEM((PLANE - 1, depth, 4, 128), F32),
            pltpu.VMEM((4, 128), F32),
            pltpu.VMEM((PLANE - 1, 4, 128), F32),
            pltpu.VMEM((2, depth, 8, 128), F32),
            pltpu.VMEM((2, depth, 8, 128), F32),
            pltpu.VMEM((2, PLANE, depth, COLBLK, 2, 128), F32),
            dma((ntile // PIECE,)),
            dma((2, 2, 2, PLANE - 1)),
            dma((2, PLANE - 1)),
            dma((2, 2, depth)),
            dma((2, 2, depth)),
            dma((2, 2, 2, PLANE - 1)),
        ],
        compiler_params=pltpu.CompilerParams(
            collective_id=0, has_side_effects=True, vmem_limit_bytes=48 << 20
        ),
    )(
        tiles,
        tile_row,
        tile_col,
        tile_count,
        first_of,
        second_of,
        cost,
        bound_vec.reshape(1, -1),
        x_start,
        y_start,
    )


def solution(mesh):
    return jax.shard_map(
        shards,
        mesh=mesh,
        in_specs=(
            P("band", None, None, None),
            P("band", None),
            P("band", None),
            P("band"),
            P("batch", "band"),
            P("band"),
            P("batch", "band"),
            P("batch", "band"),
        ),
        out_specs=(P("batch", "band"), P("batch", "band")),
        check_vma=False,
    )
```

time: 540 us -> 90 us (0.17)
  blocking collectives: 299 us -> 0 us
  waiting for transfers between devices: 99.5 us -> 0 us
  Pallas kernels: 0 us -> 80.2 us
  starting transfers between devices: 67.2 us -> 0 us
  matrix products: 28.9 us -> 0 us
  other arithmetic: 21.6 us -> 0.79 us
  between operations: 15 us -> 1.31 us
    psum x1 -> x0, blocking collectives: 253 us -> none  [shards(): primal_step, dual_step = lax.psum((primal_step, dual_step), 'band')]
    pallas_call x0 -> x1, Pallas kernels: none -> 80.2 us  [shards(): pl.pallas_call(kernel, out_shape=(jax.ShapeDtypeStruct((2, COLBLK * 128),...]
    all_to_all x5 -> x0, starting transfers between devices: 67.2 us -> none  [the longest x1 20.6 us: shards(): lax.all_to_all(requests, 'band', split_axis=0, concat_axis=0, tiled=True)]
    pmax x1 -> x0, waiting for transfers between devices: 54.1 us -> none  [shards(): col_send = lax.pmax(col_send, 'batch')]
    all_to_all x5 -> x0, waiting for transfers between devices: 45.4 us -> none  [the longest x1 20.4 us: forward(): lax.all_to_all(replies, 'band', split_axis=0, concat_axis=0, tiled=True)]
    all_to_all x1 -> x0, blocking collectives: 37 us -> none  [forward(): lax.all_to_all(replies, 'band', split_axis=0, concat_axis=0, tiled=True)]
    dot_general x12 -> x0, matrix products: 28.9 us -> none  [the longest x2 16.8 us: forward(): product = jnp.einsum('tij,tkj->tki', widened, picked, precision=high)]
    scatter-add x2 -> x0, other arithmetic: 9.99 us -> none  [adjoint(): outgoing = jnp.zeros((overflow, columns, tile_edge), jnp.float32).at[slot...]
  transfers between devices with their start and end apart: 6 -> 0, of which waited for: 4 -> 0; matrix products, arithmetic and copies ran while one was open for 4% -> 0% of each run, Pallas kernels for 0% -> 0%
where the time goes in v2:
time: 90 us; the launch traced here: 89.7 us
  Pallas kernels  80.2 us (89%)
  local copies, waits for them, and re-layouts  7.39 us (8%)
  between operations  1.31 us (1%)
    pallas_call x1, Pallas kernels, shards(): pl.pallas_call(kernel, out_shape=(jax.ShapeDtypeStruct((2, COLBLK * 128),...  80.2 us
    unnamed x16, local copies, waits for them, and re-layouts  7.39 us

profile of v2, /device:TPU:1, one launch (start us, length us, event | category | flops | bytes accessed | tf_op | source)
XLA Modules:
  0.0 89.7 jit_solution(12312758333402589778)
XLA Ops:
  1.3 0.7 fusion.1
  1.9 0.1 select_reduce_fusion
  2.1 0.0 copy-start
  2.1 2.2 %copy-done = bf16[1,128,128,128]{3,2,1,0:T(8,128)(2,1)S(1)} copy-done((bf16[1,128,128,128]{3,2,1,0:T(8,128)(2,1)S(1)}, bf16[1,128,128,128]{3,2,1,0:T(8,128)(2,1)}, u32[]{:S(2)}) %copy-start) | copy-done | bytes 4194328
  4.3 0.0 copy-start.1
  4.3 0.7 copy-done.1
  5.0 0.0 copy-start.2
  5.0 0.7 copy-done.2
  5.6 0.0 copy-start.3
  5.6 0.7 copy-done.3
  6.3 0.0 copy-start.4
  6.3 0.7 copy-done.4
  7.0 0.0 copy-start.5
  7.0 0.7 copy-done.5
  7.7 0.0 copy-start.6
  7.7 0.7 copy-done.6
  8.3 80.2 %shard_map.95 = (f32[2,256]{1,0:T(2,128)S(1)}, f32[2,512]{1,0:T(2,128)S(1)}) custom-call(bf16[1,128,128,128]{3,2,1,0:T(8,128)(2,1)S(1)} %copy-done, s32[1,128]{1,0:T(1,128)S(1)} %copy-done.5, s32[1,128]{1,0:T(1,128)S(1)} %copy-done.6, s32[1]{0:T(128)} %copy.12.tile_count, s32[128]{0:T(128)S(1)} %get-tuple-element.3.first_of, ...), custom_call_target="tpu_custom_call" | custom-call | tf_op jit(solution)/shard_map/pallas_call | solution.py:418
  88.5 0.6 copy.13
  89.1 0.6 copy.14
  (2 shorter events, 0.0 us)
Async XLA Ops:
  2.1 2.2 %copy-start = (bf16[1,128,128,128]{3,2,1,0:T(8,128)(2,1)S(1)}, bf16[1,128,128,128]{3,2,1,0:T(8,128)(2,1)}, u32[]{:S(2)}) copy-start(bf16[1,128,128,128]{3,2,1,0:T(8,128)(2,1)} %tiles_in.1) | copy-start | bytes 12582916
  4.3 0.7 copy-start.1
  5.0 0.7 copy-start.2
  5.6 0.7 copy-start.3
  6.3 0.7 copy-start.4
  7.0 0.7 copy-start.5
  7.7 0.7 copy-start.6

commit v3 on v2

v3 whole, which is shorter than its diff:
```python
import jax
import jax.numpy as jnp
from jax import lax
from jax.experimental import pallas as pl
from jax.experimental.pallas import tpu as pltpu
from jax.sharding import PartitionSpec as P

ROWBLK = 4
COLBLK = 2
CORES = 2
RING = 4
PLANE = CORES * RING
UNROLL = 32
PIECE = 32

step_size = 0.0625
MESH = pl.DeviceIdType.MESH
F32 = jnp.float32
BF16 = jnp.bfloat16


def rows8():
    return lax.broadcasted_iota(jnp.int32, (8, 128), 0)


def split_parts(value):
    high = value.astype(BF16).astype(F32)
    return jnp.concatenate([high, value - high], axis=0).astype(BF16)


def slot_of(offset, depth):
    if isinstance(offset, int):
        return max(2 * offset - 1, 0) if offset <= depth // 2 else 2 * (depth - offset)
    ahead = jnp.maximum(2 * offset - 1, 0)
    return jnp.where(offset <= depth // 2, ahead, 2 * (depth - offset))


def offset_of(slot, depth):
    return (slot + 1) // 2 if slot % 2 == 1 else (depth - slot // 2) % depth


def dual_rows(ref):
    return jnp.concatenate(
        [ref[k : k + 1, r * 128 : (r + 1) * 128] for k in range(2) for r in range(ROWBLK)], axis=0
    )


def bound_rows(ref):
    rows = [ref[0:1, r * 128 : (r + 1) * 128] for r in range(ROWBLK)]
    return jnp.concatenate(rows + rows, axis=0)


def primal_rows(ref):
    return jnp.concatenate(
        [ref[k : k + 1, c * 128 : (c + 1) * 128] for c in range(COLBLK) for k in range(2)], axis=0
    )


def fill_weights(weighted, table):
    row = rows8()
    for r in range(ROWBLK):
        first = jnp.broadcast_to(weighted[r : r + 1], (8, 128))
        second = jnp.broadcast_to(weighted[ROWBLK + r : ROWBLK + r + 1], (8, 128))
        for c in range(COLBLK):
            entry = jnp.where(row == 2 * c, first, jnp.where(row == 2 * c + 1, second, 0.0))
            table[r * COLBLK + c] = split_parts(entry)
    table[ROWBLK * COLBLK] = jnp.zeros((16, 128), BF16)


def fill_index(rows, cols, count, depth, y, z, core, index):
    ntile = rows.shape[1]
    lane = lax.broadcasted_iota(jnp.int32, (8, ntile), 1)
    live = lane < count
    row = jnp.broadcast_to(rows, (8, ntile))
    col = jnp.broadcast_to(cols, (8, ntile))
    part = col & 1
    owner = col >> 1
    side = (owner + core) & 1
    turn = ((owner >> 1) + RING - y) & (RING - 1)
    far = ((owner >> 3) + depth - z) & (depth - 1)
    slot = jnp.where(far <= depth // 2, jnp.maximum(2 * far - 1, 0), 2 * (depth - far))
    place = (side * RING + turn) * depth + slot
    at = lax.broadcasted_iota(jnp.int32, (8, ntile), 0)
    index[0, :, 0:ntile] = jnp.where(
        at == 0,
        jnp.where(live, row, ROWBLK),
        jnp.where(
            at == 1,
            jnp.where(live, row * COLBLK + part, ROWBLK * COLBLK),
            place * COLBLK + part,
        ),
    )
    places = PLANE * depth
    wide = jnp.broadcast_to(jnp.where(live, place, -1)[0:1], (128, ntile)).astype(F32)
    match = jnp.transpose(wide) == lax.broadcasted_iota(jnp.int32, (ntile, 128), 1).astype(F32)
    tile = lax.broadcasted_iota(jnp.int32, (ntile, 128), 0)
    first = jnp.min(jnp.where(match, tile, ntile), axis=0, keepdims=True)
    second = jnp.max(jnp.where(match, tile, -1), axis=0, keepdims=True)
    second = jnp.where(second > first, second, ntile)
    at = lax.broadcasted_iota(jnp.int32, (8, 128), 0)
    index[1] = jnp.where(
        at == 0, jnp.broadcast_to(first, (8, 128)), jnp.broadcast_to(second, (8, 128))
    )


def kernel(
    tiles_in,
    row_in,
    col_in,
    tile_count,
    cost_in,
    bound_in,
    x_in,
    y_in,
    x_out,
    y_out,
    tiles,
    flipped,
    spread,
    table,
    parts,
    wide_out,
    wide_core,
    wide_y,
    slim_out,
    slim_core,
    slim_y,
    steps_out,
    steps_in,
    reduced,
    line_in,
    gathered,
    row_vmem,
    col_vmem,
    cost,
    bound_vec,
    x_start,
    y_start,
    tile_row,
    index_vmem,
    index,
    tile_sem,
    small_sem,
    core_sem,
    ring_sem,
    steps_sem,
    line_sem,
    back_line_sem,
    back_plane_sem,
):
    ntile = tiles.shape[0]
    depth = reduced.shape[1]
    edges = (0, depth // 2, depth - depth // 4, depth) if depth >= 8 else (0, depth // 2, depth)
    chunks = tuple(zip(edges[:-1], edges[1:]))
    nchunk = len(chunks)
    me = lax.axis_index("band")
    z = me // PLANE
    y = (me // CORES) % RING
    core = me % CORES
    plane = [(a, b) for a in range(CORES) for b in range(RING) if (a, b) != (0, 0)]
    plane_peer = {
        (a, b): z * PLANE + ((y + b) % RING) * CORES + (core + a) % CORES for a, b in plane
    }
    line_peer = {d: ((z + d) % depth) * PLANE + me % PLANE for d in range(1, depth)}
    count = tile_count[0]
    row = rows8()
    started = []

    barrier = pltpu.get_barrier_semaphore()
    for band in list(plane_peer.values()) + list(line_peer.values()):
        pl.semaphore_signal(barrier, inc=1, device_id={"band": band}, device_id_type=MESH)

    def piece_copy(i):
        at = pl.ds(i * PIECE, PIECE)
        return pltpu.make_async_copy(tiles_in.at[0, at], tiles.at[at], tile_sem.at[i])

    small = [
        pltpu.make_async_copy(src, dst, small_sem.at[i])
        for i, (src, dst) in enumerate(
            (
                (row_in, tile_row),
                (row_in, row_vmem),
                (col_in, col_vmem),
                (y_in, y_start),
                (bound_in, bound_vec),
                (x_in, x_start),
                (cost_in, cost),
            )
        )
    ]
    index_copy = pltpu.make_async_copy(index_vmem, index, small_sem.at[len(small)])
    for copy in small[:3]:
        copy.start()
    for i in range(ntile // PIECE):
        piece_copy(i).start()
    for copy in small[3:]:
        copy.start()
    small[1].wait()
    small[2].wait()
    fill_index(row_vmem[...], col_vmem[...], count, depth, y, z, core, index_vmem)
    index_copy.start()
    small[0].wait()

    def send(src, dst, send_sem, recv_sem, band):
        copy = pltpu.make_async_remote_copy(
            src_ref=src,
            dst_ref=dst,
            send_sem=send_sem,
            recv_sem=recv_sem,
            device_id={"band": band},
            device_id_type=MESH,
        )
        copy.start()
        started.append(copy)
        return copy

    def live_row(t):
        return jnp.where(t < count, tile_row[0, t], ROWBLK)

    def peak_piece(i, peaks):
        piece_copy(i).wait()

        def peak_body(step, peaks):
            peaks = list(peaks)
            for u in range(UNROLL):
                t = i * PIECE + step * UNROLL + u
                r = live_row(t)
                size = jnp.abs(tiles[t])
                for k in range(ROWBLK):
                    peaks[k] = jnp.maximum(peaks[k], jnp.where(r == k, size, jnp.zeros_like(size)))
            return tuple(peaks)

        return lax.fori_loop(0, PIECE // UNROLL, peak_body, peaks)

    peaks = lax.fori_loop(
        0, ntile // PIECE, peak_piece, (jnp.zeros((128, 128), BF16),) * ROWBLK
    )
    lines = []
    for r in range(ROWBLK):
        peak = jnp.max(peaks[r].astype(F32), axis=1, keepdims=True)
        scale = jnp.broadcast_to(lax.rsqrt(peak), (128, 128))
        spread[r] = scale
        lines.append(jnp.transpose(scale)[0:1])
    spread[ROWBLK] = jnp.zeros((128, 128), F32)
    rscale = jnp.concatenate(lines + lines, axis=0)
    small[3].wait()
    small[4].wait()
    start = dual_rows(y_start)
    sbound = bound_rows(bound_vec) * rscale
    fill_weights(start * rscale, table)
    parts[ntile] = jnp.zeros((8, 128), F32)
    index_copy.wait()

    def scale_body(step, carry):
        for u in range(UNROLL):
            t = step * UNROLL + u
            entry = index[0, 1, t]
            block = tiles[t]
            peak = jnp.max(
                jnp.abs(block.astype(F32)) * spread[index[0, 0, t]], axis=0, keepdims=True
            )
            peak = jnp.broadcast_to(peak, (8, 128))
            product = jnp.dot(table[entry], block, preferred_element_type=F32)
            parts[t] = jnp.where(
                row < 4,
                product[0:8] + product[8:16],
                jnp.where(row == 4 + entry % COLBLK, peak, 0.0),
            )
        return carry

    lax.fori_loop(0, ntile // UNROLL, scale_body, 0)

    def adjoint_body(step, carry):
        for u in range(UNROLL):
            t = step * UNROLL + u
            product = jnp.dot(table[index[0, 1, t]], tiles[t], preferred_element_type=F32)
            parts[t] = product[0:8] + product[8:16]
        return carry

    def place_parts(store):
        def body(slot, carry):
            for a in range(CORES):
                for b in range(RING):
                    at = (a * RING + b) * depth + slot
                    store(a, b, slot, parts[index[1, 0, at]], parts[index[1, 1, at]])
            return carry

        lax.fori_loop(0, depth, body, 0)

    def store_wide(a, b, slot, first, second):
        wide_out[a, b, slot] = jnp.where(row < 4, first + second, jnp.maximum(first, second))

    def store_slim(a, b, slot, first, second):
        slim_out[a, b, slot] = (first + second)[0:4]

    def back_of(slot):
        return slot_of((depth - offset_of(slot, depth)) % depth, depth)

    def reduce_scatter(turn, out, from_core, from_y, combine, steps=None):
        order = tuple(range(nchunk))[::-1]
        sent = {}
        for n in order:
            at = pl.ds(chunks[n][0], chunks[n][1] - chunks[n][0])
            sent[n] = send(
                out.at[1, :, at],
                from_core.at[:, at],
                core_sem.at[turn, 0, n],
                core_sem.at[turn, 1, n],
                plane_peer[1, 0],
            )
        if steps is not None:
            steps_out[...] = steps
            for i, peer in enumerate(plane):
                sent["steps", i] = send(
                    steps_out,
                    steps_in.at[i],
                    steps_sem.at[0, i],
                    steps_sem.at[1, i],
                    plane_peer[peer],
                )
        for n in order:
            lo, hi = chunks[n]
            at = pl.ds(lo, hi - lo)
            sent[n].wait_recv()
            for b in range(RING):
                from_core[b, lo:hi] = combine(out[0, b, lo:hi], from_core[b, lo:hi])
            for b in range(1, RING):
                sent[n, b] = send(
                    from_core.at[b, at],
                    from_y.at[b - 1, at],
                    ring_sem.at[turn, 0, n, b - 1],
                    ring_sem.at[turn, 1, n, b - 1],
                    plane_peer[0, b],
                )
        if steps is not None:
            for i in range(len(plane)):
                sent["steps", i].wait_recv()
                steps = steps + steps_in[i]
        line = {}
        for n in order:
            lo, hi = chunks[n]
            total = from_core[0, lo:hi]
            for b in range(1, RING):
                sent[n, b].wait_recv()
                total = combine(total, from_y[b - 1, lo:hi])
            if steps is None:
                reduced[turn, lo:hi] = total
            else:
                reduced[turn, lo:hi, 0:4] = total
                reduced[turn, lo:hi, 4:8] = jnp.broadcast_to(steps[None], (hi - lo, 4, 128))
            for slot in range(hi - 1, max(lo, 1) - 1, -1):
                back = back_of(slot)
                line[back] = send(
                    reduced.at[turn, slot],
                    line_in.at[turn, back],
                    line_sem.at[turn, 0, slot],
                    line_sem.at[turn, 1, back],
                    line_peer[offset_of(slot, depth)],
                )
        return line

    def collect(turn, line, combine):
        mine = reduced[turn, 0]
        for slot in range(1, depth):
            line[slot].wait_recv()
            mine = combine(mine, line_in[turn, slot])
        return mine

    def all_gather(turn, block):
        for c in range(COLBLK):
            gathered[turn, 0, 0, c] = block[2 * c : 2 * c + 2]
        line = {}
        for slot in range(depth - 1, 0, -1):
            back = back_of(slot)
            line[back] = send(
                gathered.at[turn, 0, 0],
                gathered.at[turn, 0, back],
                back_line_sem.at[turn, 0, slot],
                back_line_sem.at[turn, 1, back],
                line_peer[offset_of(slot, depth)],
            )
        sent = []
        for n, (lo, hi) in enumerate(chunks):
            for slot in range(max(lo, 1), hi):
                line[slot].wait_recv()
            at = pl.ds(lo, hi - lo)
            for i, (a, b) in enumerate(plane):
                sent.append(
                    send(
                        gathered.at[turn, 0, at],
                        gathered.at[turn, a * RING + (RING - b) % RING, at],
                        back_plane_sem.at[turn, 0, n, i],
                        back_plane_sem.at[turn, 1, n, i],
                        plane_peer[a, b],
                    )
                )
        for copy in sent:
            copy.wait_recv()

    def forward(turn):
        def body(step, acc):
            lhs = []
            for u in range(UNROLL):
                t = step * UNROLL + u
                r = index[0, 0, t]
                at = index[0, 2, t]
                pair = gathered[turn, at // (depth * COLBLK), (at // COLBLK) % depth, at % COLBLK]
                value = jnp.where(
                    row < ROWBLK,
                    jnp.broadcast_to(pair[0:1], (8, 128)),
                    jnp.broadcast_to(pair[1:2], (8, 128)),
                )
                lhs.append(split_parts(jnp.where(row % ROWBLK == r, value, 0.0)))
            block = flipped[pl.ds(step * UNROLL, UNROLL)].reshape(UNROLL * 128, 128)
            return acc + jnp.dot(
                jnp.concatenate(lhs, axis=1), block, preferred_element_type=F32
            )

        acc = lax.fori_loop(0, ntile // UNROLL, body, jnp.zeros((16, 128), F32))
        return (acc[0:8] + acc[8:16]) * rscale

    def join(a, b):
        top = lax.broadcasted_iota(jnp.int32, a.shape, a.ndim - 2) < 4
        return jnp.where(top, a + b, jnp.maximum(a, b))

    def add(a, b):
        return a + b

    place_parts(store_wide)
    pl.semaphore_wait(barrier, len(plane_peer) + len(line_peer))
    line = reduce_scatter(0, wide_out, wide_core, wide_y, join)

    def flip_body(step, carry):
        for u in range(UNROLL):
            t = step * UNROLL + u
            flipped[t] = jnp.transpose(tiles[t])
        return carry

    lax.fori_loop(0, ntile // UNROLL, flip_body, 0)
    mine = collect(0, line, join)

    row4 = lax.broadcasted_iota(jnp.int32, (4, 128), 0)
    cscale = lax.rsqrt(
        jnp.where(
            row4 < 2,
            jnp.broadcast_to(mine[4:5], (4, 128)),
            jnp.broadcast_to(mine[5:6], (4, 128)),
        )
    )
    small[5].wait()
    small[6].wait()
    before = primal_rows(x_start)
    scost = primal_rows(cost) * cscale
    primal = jnp.maximum(0.0, before - step_size * (scost - mine[0:4] * cscale))
    all_gather(0, (2.0 * primal - before) * cscale)
    move = (primal - before) ** 2
    dual = jnp.maximum(0.0, start + step_size * (sbound - forward(0)))
    fill_weights(dual * rscale, table)
    turn = (dual - start) ** 2
    steps = jnp.concatenate(
        [
            move[0:2] + move[2:4],
            jnp.sum(turn[0:4], axis=0, keepdims=True),
            jnp.sum(turn[4:8], axis=0, keepdims=True),
        ],
        axis=0,
    )

    lax.fori_loop(0, ntile // UNROLL, adjoint_body, 0)
    place_parts(store_slim)
    mine = collect(1, reduce_scatter(1, slim_out, slim_core, slim_y, add, steps), add)
    sums = jnp.sum(mine[4:8], axis=1, keepdims=True) + 1e-06
    omega = jnp.broadcast_to(jnp.sqrt(sums[2:4] / sums[0:2]), (2, 128))
    wide = jnp.concatenate([omega, omega], axis=0)
    after = jnp.maximum(0.0, primal - (step_size / wide) * (scost - mine[0:4] * cscale))
    all_gather(1, (2.0 * after - primal) * cscale)
    for c in range(COLBLK):
        x_out[:, c * 128 : (c + 1) * 128] = after[2 * c : 2 * c + 2]
    pace = jnp.concatenate(
        [
            jnp.broadcast_to(step_size * omega[0:1], (4, 128)),
            jnp.broadcast_to(step_size * omega[1:2], (4, 128)),
        ],
        axis=0,
    )
    last = jnp.maximum(0.0, dual + pace * (sbound - forward(1)))
    for k in range(2):
        for r in range(ROWBLK):
            y_out[k : k + 1, r * 128 : (r + 1) * 128] = last[k * ROWBLK + r : k * ROWBLK + r + 1]
    for copy in started:
        copy.wait_send()


HBM = pl.BlockSpec(memory_space=pltpu.HBM)
VMEM = pl.BlockSpec(memory_space=pltpu.VMEM)
SMEM = pl.BlockSpec(memory_space=pltpu.SMEM)


def shards(tiles, tile_row, tile_col, tile_count, cost, bound_vec, x_start, y_start):
    ntile = tiles.shape[1]
    depth = lax.axis_size("band") // PLANE
    dma = pltpu.SemaphoreType.DMA
    nchunk = 3 if depth >= 8 else 2
    return pl.pallas_call(
        kernel,
        out_shape=(
            jax.ShapeDtypeStruct((2, COLBLK * 128), F32),
            jax.ShapeDtypeStruct((2, ROWBLK * 128), F32),
        ),
        in_specs=[HBM] * 3 + [SMEM] + [HBM] * 4,
        out_specs=(VMEM, VMEM),
        scratch_shapes=[
            pltpu.VMEM((ntile, 128, 128), BF16),
            pltpu.VMEM((ntile, 128, 128), BF16),
            pltpu.VMEM((ROWBLK + 1, 128, 128), F32),
            pltpu.VMEM((ROWBLK * COLBLK + 1, 16, 128), BF16),
            pltpu.VMEM((ntile + 1, 8, 128), F32),
            pltpu.VMEM((CORES, RING, depth, 8, 128), F32),
            pltpu.VMEM((RING, depth, 8, 128), F32),
            pltpu.VMEM((RING - 1, depth, 8, 128), F32),
            pltpu.VMEM((CORES, RING, depth, 4, 128), F32),
            pltpu.VMEM((RING, depth, 4, 128), F32),
            pltpu.VMEM((RING - 1, depth, 4, 128), F32),
            pltpu.VMEM((4, 128), F32),
            pltpu.VMEM((PLANE - 1, 4, 128), F32),
            pltpu.VMEM((2, depth, 8, 128), F32),
            pltpu.VMEM((2, depth, 8, 128), F32),
            pltpu.VMEM((2, PLANE, depth, COLBLK, 2, 128), F32),
            pltpu.VMEM((1, ntile), jnp.int32),
            pltpu.VMEM((1, ntile), jnp.int32),
            pltpu.VMEM((2, COLBLK * 128), F32),
            pltpu.VMEM((1, ROWBLK * 128), F32),
            pltpu.VMEM((2, COLBLK * 128), F32),
            pltpu.VMEM((2, ROWBLK * 128), F32),
            pltpu.SMEM((1, ntile), jnp.int32),
            pltpu.VMEM((2, 8, 128), jnp.int32),
            pltpu.SMEM((2, 8, 128), jnp.int32),
            dma((ntile // PIECE,)),
            dma((8,)),
            dma((2, 2, nchunk)),
            dma((2, 2, nchunk, RING - 1)),
            dma((2, PLANE - 1)),
            dma((2, 2, depth)),
            dma((2, 2, depth)),
            dma((2, 2, nchunk, PLANE - 1)),
        ],
        compiler_params=pltpu.CompilerParams(
            collective_id=0, has_side_effects=True, vmem_limit_bytes=60 << 20
        ),
    )(
        tiles,
        tile_row,
        tile_col,
        tile_count,
        cost,
        bound_vec.reshape(1, -1),
        x_start,
        y_start,
    )


def solution(mesh):
    return jax.shard_map(
        shards,
        mesh=mesh,
        in_specs=(
            P("band", None, None, None),
            P("band", None),
            P("band", None),
            P("band"),
            P("batch", "band"),
            P("band"),
            P("batch", "band"),
            P("batch", "band"),
        ),
        out_specs=(P("batch", "band"), P("batch", "band")),
        check_vma=False,
    )
```

time: 90 us -> 76.2 us (0.85)
  Pallas kernels: 80.2 us -> 72.2 us
  local copies, waits for them, and re-layouts: 7.39 us -> 2.5 us
    pallas_call x1, Pallas kernels: 80.2 us -> 72.2 us  [shards(): pl.pallas_call(kernel, out_shape=(jax.ShapeDtypeStruct((2, COLBLK * 128),...]
    unnamed x16 -> x2, local copies, waits for them, and re-layouts: 7.39 us -> 2.5 us
where the time goes in v3:
time: 76.2 us; the launch traced here: 76 us
  Pallas kernels  72.2 us (95%)
  local copies, waits for them, and re-layouts  2.5 us (3%)
  between operations  1.29 us (2%)
    pallas_call x1, Pallas kernels, shards(): pl.pallas_call(kernel, out_shape=(jax.ShapeDtypeStruct((2, COLBLK * 128),...  72.2 us
    unnamed x2, local copies, waits for them, and re-layouts  2.5 us

profile of v3, /device:TPU:1, one launch (start us, length us, event | category | flops | bytes accessed | tf_op | source)
XLA Modules:
  0.0 76.0 jit_solution(8342634839661117989)
XLA Ops:
  1.3 72.2 %shard_map.95 = (f32[2,256]{1,0:T(2,128)}, f32[2,512]{1,0:T(2,128)}) custom-call(bf16[1,128,128,128]{3,2,1,0:T(8,128)(2,1)} %tiles_in.1, s32[1,128]{1,0:T(1,128)} %row_in.1, s32[1,128]{1,0:T(1,128)} %col_in.1, s32[1]{0:T(128)S(6)} %copy.12.tile_count, f32[2,256]{1,0:T(2,128)} %cost_in.1, f32[1,512]{1,0:T(1,128)} %bitcast.1, f32[2,256]{1,0:T(2,128)} %x_in.1, ...), custom_call_target="tpu_custom_call" | custom-call | tf_op jit(solution)/shard_map/pallas_call | solution.py:504
  73.5 1.2 %copy.13 = f32[2,256]{1,0:T(2,128)} copy(f32[2,256]{1,0:T(2,128)} %get-tuple-element.4) | data formatting | bytes 4096
  74.7 1.3 %copy.14 = f32[2,512]{1,0:T(2,128)} copy(f32[2,512]{1,0:T(2,128)} %get-tuple-element.5) | data formatting | bytes 8192

commit v4 on v3

--- a/solution.py
+++ b/solution.py
@@ -122,9 +122,11 @@
     wide_out,
     wide_core,
     wide_y,
+    wide_far,
     slim_out,
     slim_core,
     slim_y,
+    slim_far,
     steps_out,
     steps_in,
     reduced,
@@ -143,16 +145,20 @@
     small_sem,
     core_sem,
     ring_sem,
+    far_sem,
     steps_sem,
     line_sem,
     back_line_sem,
     back_plane_sem,
+    back_far_sem,
 ):
     ntile = tiles.shape[0]
-    depth = reduced.shape[1]
-    edges = (0, depth // 2, depth - depth // 4, depth) if depth >= 8 else (0, depth // 2, depth)
+    depth = reduced.shape[2]
+    edges = (0, depth // 2 - 1, depth - 3) if depth >= 8 else (0, 1)
     chunks = tuple(zip(edges[:-1], edges[1:]))
     nchunk = len(chunks)
+    rim = edges[-1]
+    far = pl.ds(rim, depth - rim)
     me = lax.axis_index("band")
     z = me // PLANE
     y = (me // CORES) % RING
@@ -162,12 +168,17 @@
         (a, b): z * PLANE + ((y + b) % RING) * CORES + (core + a) % CORES for a, b in plane
     }
     line_peer = {d: ((z + d) % depth) * PLANE + me % PLANE for d in range(1, depth)}
+    cross_peer = {
+        slot: ((z + offset_of(slot, depth)) % depth) * PLANE + me % PLANE + 1 - 2 * core
+        for slot in range(rim, depth)
+    }
+    peers = list(plane_peer.values()) + list(line_peer.values()) + list(cross_peer.values())
     count = tile_count[0]
     row = rows8()
     started = []
 
     barrier = pltpu.get_barrier_semaphore()
-    for band in list(plane_peer.values()) + list(line_peer.values()):
+    for band in peers:
         pl.semaphore_signal(barrier, inc=1, device_id={"band": band}, device_id_type=MESH)
 
     def piece_copy(i):
@@ -264,7 +275,7 @@
             parts[t] = jnp.where(
                 row < 4,
                 product[0:8] + product[8:16],
-                jnp.where(row == 4 + entry % COLBLK, peak, 0.0),
+                jnp.where(row == 4 + (entry & 1), peak, 0.0),
             )
         return carry
 
@@ -296,9 +307,17 @@
     def back_of(slot):
         return slot_of((depth - offset_of(slot, depth)) % depth, depth)
 
-    def reduce_scatter(turn, out, from_core, from_y, combine, steps=None):
+    def reduce_scatter(turn, out, from_core, from_y, from_far, combine, steps=None):
         order = tuple(range(nchunk))[::-1]
         sent = {}
+        for b in range(1, RING):
+            sent["far", b] = send(
+                out.at[:, b, far],
+                from_far.at[b - 1],
+                far_sem.at[turn, 0, b - 1],
+                far_sem.at[turn, 1, b - 1],
+                plane_peer[0, b],
+            )
         for n in order:
             at = pl.ds(chunks[n][0], chunks[n][1] - chunks[n][0])
             sent[n] = send(
@@ -332,38 +351,58 @@
                     ring_sem.at[turn, 1, n, b - 1],
                     plane_peer[0, b],
                 )
+
+        def keep(a, lo, hi, total):
+            if steps is None:
+                reduced[turn, a, lo:hi] = total
+            else:
+                reduced[turn, a, lo:hi, 0:4] = total
+                extra = steps if a == 0 else jnp.zeros_like(steps)
+                reduced[turn, a, lo:hi, 4:8] = jnp.broadcast_to(extra[None], (hi - lo, 4, 128))
+
         if steps is not None:
             for i in range(len(plane)):
                 sent["steps", i].wait_recv()
                 steps = steps + steps_in[i]
+        for b in range(1, RING):
+            sent["far", b].wait_recv()
+        for a in range(CORES):
+            total = out[a, 0, rim:depth]
+            for b in range(1, RING):
+                total = combine(total, from_far[b - 1, a])
+            keep(a, rim, depth, total)
         line = {}
+
+        def along(a, slot):
+            back = back_of(slot)
+            line[a, back] = send(
+                reduced.at[turn, a, slot],
+                line_in.at[turn, a, back],
+                line_sem.at[turn, a, 0, slot],
+                line_sem.at[turn, a, 1, back],
+                cross_peer[slot] if a else line_peer[offset_of(slot, depth)],
+            )
+
+        for slot in range(depth - 1, rim - 1, -1):
+            for a in range(CORES):
+                along(a, slot)
         for n in order:
             lo, hi = chunks[n]
             total = from_core[0, lo:hi]
             for b in range(1, RING):
                 sent[n, b].wait_recv()
                 total = combine(total, from_y[b - 1, lo:hi])
-            if steps is None:
-                reduced[turn, lo:hi] = total
-            else:
-                reduced[turn, lo:hi, 0:4] = total
-                reduced[turn, lo:hi, 4:8] = jnp.broadcast_to(steps[None], (hi - lo, 4, 128))
+            keep(0, lo, hi, total)
             for slot in range(hi - 1, max(lo, 1) - 1, -1):
-                back = back_of(slot)
-                line[back] = send(
-                    reduced.at[turn, slot],
-                    line_in.at[turn, back],
-                    line_sem.at[turn, 0, slot],
-                    line_sem.at[turn, 1, back],
-                    line_peer[offset_of(slot, depth)],
-                )
+                along(0, slot)
         return line
 
     def collect(turn, line, combine):
-        mine = reduced[turn, 0]
+        mine = reduced[turn, 0, 0]
         for slot in range(1, depth):
-            line[slot].wait_recv()
-            mine = combine(mine, line_in[turn, slot])
+            for a in range(CORES if slot >= rim else 1):
+                line[a, slot].wait_recv()
+                mine = combine(mine, line_in[turn, a, slot])
         return mine
 
     def all_gather(turn, block):
@@ -372,30 +411,47 @@
         line = {}
         for slot in range(depth - 1, 0, -1):
             back = back_of(slot)
-            line[back] = send(
-                gathered.at[turn, 0, 0],
-                gathered.at[turn, 0, back],
-                back_line_sem.at[turn, 0, slot],
-                back_line_sem.at[turn, 1, back],
-                line_peer[offset_of(slot, depth)],
-            )
+            for a in range(CORES if slot >= rim else 1):
+                line[a, back] = send(
+                    gathered.at[turn, 0, 0, pl.ds(0, COLBLK)],
+                    gathered.at[turn, a, 0, pl.ds(back * COLBLK, COLBLK)],
+                    back_line_sem.at[turn, a, 0, slot],
+                    back_line_sem.at[turn, a, 1, back],
+                    cross_peer[slot] if a else line_peer[offset_of(slot, depth)],
+                )
         sent = []
         for n, (lo, hi) in enumerate(chunks):
             for slot in range(max(lo, 1), hi):
-                line[slot].wait_recv()
-            at = pl.ds(lo, hi - lo)
+                line[0, slot].wait_recv()
+            at = pl.ds(lo * COLBLK, (hi - lo) * COLBLK)
             for i, (a, b) in enumerate(plane):
                 sent.append(
                     send(
-                        gathered.at[turn, 0, at],
-                        gathered.at[turn, a * RING + (RING - b) % RING, at],
+                        gathered.at[turn, 0, 0, at],
+                        gathered.at[turn, a, (RING - b) % RING, at],
                         back_plane_sem.at[turn, 0, n, i],
                         back_plane_sem.at[turn, 1, n, i],
                         plane_peer[a, b],
                     )
                 )
+        edge = pl.ds(rim * COLBLK, (depth - rim) * COLBLK)
+        for slot in range(rim, depth):
+            for a in range(CORES):
+                line[a, slot].wait_recv()
+        for b in range(1, RING):
+            sent.append(
+                send(
+                    gathered.at[turn, :, 0, edge],
+                    gathered.at[turn, :, RING - b, edge],
+                    back_far_sem.at[turn, 0, b - 1],
+                    back_far_sem.at[turn, 1, b - 1],
+                    plane_peer[0, b],
+                )
+            )
         for copy in sent:
             copy.wait_recv()
+
+    bits = (depth * COLBLK).bit_length() - 1
 
     def forward(turn):
         def body(step, acc):
@@ -404,7 +460,8 @@
                 t = step * UNROLL + u
                 r = index[0, 0, t]
                 at = index[0, 2, t]
-                pair = gathered[turn, at // (depth * COLBLK), (at // COLBLK) % depth, at % COLBLK]
+                side = at >> (bits + 2)
+                pair = gathered[turn, side, (at >> bits) & (RING - 1), at & (depth * COLBLK - 1)]
                 value = jnp.where(
                     row < ROWBLK,
                     jnp.broadcast_to(pair[0:1], (8, 128)),
@@ -427,8 +484,8 @@
         return a + b
 
     place_parts(store_wide)
-    pl.semaphore_wait(barrier, len(plane_peer) + len(line_peer))
-    line = reduce_scatter(0, wide_out, wide_core, wide_y, join)
+    pl.semaphore_wait(barrier, len(peers))
+    line = reduce_scatter(0, wide_out, wide_core, wide_y, wide_far, join)
 
     def flip_body(step, carry):
         for u in range(UNROLL):
@@ -468,7 +525,10 @@
 
     lax.fori_loop(0, ntile // UNROLL, adjoint_body, 0)
     place_parts(store_slim)
-    mine = collect(1, reduce_scatter(1, slim_out, slim_core, slim_y, add, steps), add)
+    line = reduce_scatter(
+        1, slim_out, slim_core, slim_y, slim_far, add, steps
+    )
+    mine = collect(1, line, add)
     sums = jnp.sum(mine[4:8], axis=1, keepdims=True) + 1e-06
     omega = jnp.broadcast_to(jnp.sqrt(sums[2:4] / sums[0:2]), (2, 128))
     wide = jnp.concatenate([omega, omega], axis=0)
@@ -500,7 +560,7 @@
     ntile = tiles.shape[1]
     depth = lax.axis_size("band") // PLANE
     dma = pltpu.SemaphoreType.DMA
-    nchunk = 3 if depth >= 8 else 2
+    nchunk, rim = (2, depth - 3) if depth >= 8 else (1, 1)
     return pl.pallas_call(
         kernel,
         out_shape=(
@@ -518,14 +578,16 @@
             pltpu.VMEM((CORES, RING, depth, 8, 128), F32),
             pltpu.VMEM((RING, depth, 8, 128), F32),
             pltpu.VMEM((RING - 1, depth, 8, 128), F32),
+            pltpu.VMEM((RING - 1, CORES, depth - rim, 8, 128), F32),
             pltpu.VMEM((CORES, RING, depth, 4, 128), F32),
             pltpu.VMEM((RING, depth, 4, 128), F32),
             pltpu.VMEM((RING - 1, depth, 4, 128), F32),
+            pltpu.VMEM((RING - 1, CORES, depth - rim, 4, 128), F32),
             pltpu.VMEM((4, 128), F32),
             pltpu.VMEM((PLANE - 1, 4, 128), F32),
-            pltpu.VMEM((2, depth, 8, 128), F32),
-            pltpu.VMEM((2, depth, 8, 128), F32),
-            pltpu.VMEM((2, PLANE, depth, COLBLK, 2, 128), F32),
+            pltpu.VMEM((2, CORES, depth, 8, 128), F32),
+            pltpu.VMEM((2, CORES, depth, 8, 128), F32),
+            pltpu.VMEM((2, CORES, RING, depth * COLBLK, 2, 128), F32),
             pltpu.VMEM((1, ntile), jnp.int32),
             pltpu.VMEM((1, ntile), jnp.int32),
             pltpu.VMEM((2, COLBLK * 128), F32),
@@ -539,10 +601,12 @@
             dma((8,)),
             dma((2, 2, nchunk)),
             dma((2, 2, nchunk, RING - 1)),
+            dma((2, 2, RING - 1)),
             dma((2, PLANE - 1)),
-            dma((2, 2, depth)),
-            dma((2, 2, depth)),
+            dma((2, CORES, 2, depth)),
+            dma((2, CORES, 2, depth)),
             dma((2, 2, nchunk, PLANE - 1)),
+            dma((2, 2, RING - 1)),
         ],
         compiler_params=pltpu.CompilerParams(
             collective_id=0, has_side_effects=True, vmem_limit_bytes=60 << 20

time: 76.2 us -> 74.1 us (0.972)
  Pallas kernels: 72.2 us -> 70.1 us
    pallas_call x1, Pallas kernels: 72.2 us -> 70.1 us  [shards(): pl.pallas_call(kernel, out_shape=(jax.ShapeDtypeStruct((2, COLBLK * 128),...]
where the time goes in v4:
time: 74.1 us; the launch traced here: 73.9 us
  Pallas kernels  70.1 us (95%)
  local copies, waits for them, and re-layouts  2.5 us (3%)
  between operations  1.29 us (2%)
    pallas_call x1, Pallas kernels, shards(): pl.pallas_call(kernel, out_shape=(jax.ShapeDtypeStruct((2, COLBLK * 128),...  70.1 us
    unnamed x2, local copies, waits for them, and re-layouts  2.5 us

profile of v4, /device:TPU:1, one launch (start us, length us, event | category | flops | bytes accessed | tf_op | source)
XLA Modules:
  0.0 73.9 jit_solution(8804843645744016759)
XLA Ops:
  1.3 70.1 %shard_map.95 = (f32[2,256]{1,0:T(2,128)}, f32[2,512]{1,0:T(2,128)}) custom-call(bf16[1,128,128,128]{3,2,1,0:T(8,128)(2,1)} %tiles_in.1, s32[1,128]{1,0:T(1,128)} %row_in.1, s32[1,128]{1,0:T(1,128)} %col_in.1, s32[1]{0:T(128)S(6)} %copy.12.tile_count, f32[2,256]{1,0:T(2,128)} %cost_in.1, f32[1,512]{1,0:T(1,128)} %bitcast.1, f32[2,256]{1,0:T(2,128)} %x_in.1, ...), custom_call_target="tpu_custom_call" | custom-call | tf_op jit(solution)/shard_map/pallas_call | solution.py:564
  71.4 1.2 %copy.13 = f32[2,256]{1,0:T(2,128)} copy(f32[2,256]{1,0:T(2,128)} %get-tuple-element.4) | data formatting | bytes 4096
  72.6 1.3 %copy.14 = f32[2,512]{1,0:T(2,128)} copy(f32[2,512]{1,0:T(2,128)} %get-tuple-element.5) | data formatting | bytes 8192

commit v5 on v4

--- a/solution.py
+++ b/solution.py
@@ -10,8 +10,8 @@
 CORES = 2
 RING = 4
 PLANE = CORES * RING
-UNROLL = 32
-PIECE = 32
+UNROLL = 64
+PIECE = 64
 
 step_size = 0.0625
 MESH = pl.DeviceIdType.MESH
@@ -225,6 +225,12 @@
         started.append(copy)
         return copy
 
+    def drain(kept=0):
+        done = started[: len(started) - kept]
+        del started[: len(done)]
+        for copy in done:
+            copy.wait_send()
+
     def live_row(t):
         return jnp.where(t < count, tile_row[0, t], ROWBLK)
 
@@ -288,7 +294,7 @@
             parts[t] = product[0:8] + product[8:16]
         return carry
 
-    def place_parts(store):
+    def place_parts(store, lo, hi):
         def body(slot, carry):
             for a in range(CORES):
                 for b in range(RING):
@@ -296,7 +302,7 @@
                     store(a, b, slot, parts[index[1, 0, at]], parts[index[1, 1, at]])
             return carry
 
-        lax.fori_loop(0, depth, body, 0)
+        lax.fori_loop(lo, hi, body, 0)
 
     def store_wide(a, b, slot, first, second):
         wide_out[a, b, slot] = jnp.where(row < 4, first + second, jnp.maximum(first, second))
@@ -307,9 +313,26 @@
     def back_of(slot):
         return slot_of((depth - offset_of(slot, depth)) % depth, depth)
 
-    def reduce_scatter(turn, out, from_core, from_y, from_far, combine, steps=None):
+    def reduce_scatter(turn, store, out, from_core, from_y, from_far, combine, steps=None):
         order = tuple(range(nchunk))[::-1]
         sent = {}
+
+        def send_steps(kind, b):
+            sent["steps", kind, b] = send(
+                steps_out.at[kind],
+                steps_in.at[kind, b],
+                steps_sem.at[0, kind, b],
+                steps_sem.at[1, kind, b],
+                plane_peer[0, b] if b else plane_peer[1, 0],
+            )
+
+        place_parts(store, rim, depth)
+        if steps is not None:
+            steps_out[0] = steps
+            for b in range(RING):
+                send_steps(0, b)
+        else:
+            pl.semaphore_wait(barrier, len(peers))
         for b in range(1, RING):
             sent["far", b] = send(
                 out.at[:, b, far],
@@ -320,6 +343,7 @@
             )
         for n in order:
             at = pl.ds(chunks[n][0], chunks[n][1] - chunks[n][0])
+            place_parts(store, *chunks[n])
             sent[n] = send(
                 out.at[1, :, at],
                 from_core.at[:, at],
@@ -328,15 +352,11 @@
                 plane_peer[1, 0],
             )
         if steps is not None:
-            steps_out[...] = steps
-            for i, peer in enumerate(plane):
-                sent["steps", i] = send(
-                    steps_out,
-                    steps_in.at[i],
-                    steps_sem.at[0, i],
-                    steps_sem.at[1, i],
-                    plane_peer[peer],
-                )
+            sent["steps", 0, 0].wait_recv()
+            both = steps + steps_in[0, 0]
+            steps_out[1] = both
+            for b in range(1, RING):
+                send_steps(1, b)
         for n in order:
             lo, hi = chunks[n]
             at = pl.ds(lo, hi - lo)
@@ -352,25 +372,24 @@
                     plane_peer[0, b],
                 )
 
-        def keep(a, lo, hi, total):
-            if steps is None:
+        def keep(a, lo, hi, total, extra):
+            if extra is None:
                 reduced[turn, a, lo:hi] = total
             else:
                 reduced[turn, a, lo:hi, 0:4] = total
-                extra = steps if a == 0 else jnp.zeros_like(steps)
                 reduced[turn, a, lo:hi, 4:8] = jnp.broadcast_to(extra[None], (hi - lo, 4, 128))
 
         if steps is not None:
-            for i in range(len(plane)):
-                sent["steps", i].wait_recv()
-                steps = steps + steps_in[i]
+            for b in range(1, RING):
+                sent["steps", 0, b].wait_recv()
+                steps = steps + steps_in[0, b]
         for b in range(1, RING):
             sent["far", b].wait_recv()
         for a in range(CORES):
             total = out[a, 0, rim:depth]
             for b in range(1, RING):
                 total = combine(total, from_far[b - 1, a])
-            keep(a, rim, depth, total)
+            keep(a, rim, depth, total, steps)
         line = {}
 
         def along(a, slot):
@@ -386,13 +405,18 @@
         for slot in range(depth - 1, rim - 1, -1):
             for a in range(CORES):
                 along(a, slot)
+        if steps is not None:
+            for b in range(1, RING):
+                sent["steps", 1, b].wait_recv()
+                both = both + steps_in[1, b]
+            steps = both
         for n in order:
             lo, hi = chunks[n]
             total = from_core[0, lo:hi]
             for b in range(1, RING):
                 sent[n, b].wait_recv()
                 total = combine(total, from_y[b - 1, lo:hi])
-            keep(0, lo, hi, total)
+            keep(0, lo, hi, total, steps)
             for slot in range(hi - 1, max(lo, 1) - 1, -1):
                 along(0, slot)
         return line
@@ -419,6 +443,7 @@
                     back_line_sem.at[turn, a, 1, back],
                     cross_peer[slot] if a else line_peer[offset_of(slot, depth)],
                 )
+        drain(len(line))
         sent = []
         for n, (lo, hi) in enumerate(chunks):
             for slot in range(max(lo, 1), hi):
@@ -448,6 +473,7 @@
                     plane_peer[0, b],
                 )
             )
+        drain(len(sent))
         for copy in sent:
             copy.wait_recv()
 
@@ -483,9 +509,7 @@
     def add(a, b):
         return a + b
 
-    place_parts(store_wide)
-    pl.semaphore_wait(barrier, len(peers))
-    line = reduce_scatter(0, wide_out, wide_core, wide_y, wide_far, join)
+    line = reduce_scatter(0, store_wide, wide_out, wide_core, wide_y, wide_far, join)
 
     def flip_body(step, carry):
         for u in range(UNROLL):
@@ -524,9 +548,8 @@
     )
 
     lax.fori_loop(0, ntile // UNROLL, adjoint_body, 0)
-    place_parts(store_slim)
     line = reduce_scatter(
-        1, slim_out, slim_core, slim_y, slim_far, add, steps
+        1, store_slim, slim_out, slim_core, slim_y, slim_far, add, steps
     )
     mine = collect(1, line, add)
     sums = jnp.sum(mine[4:8], axis=1, keepdims=True) + 1e-06
@@ -547,8 +570,7 @@
     for k in range(2):
         for r in range(ROWBLK):
             y_out[k : k + 1, r * 128 : (r + 1) * 128] = last[k * ROWBLK + r : k * ROWBLK + r + 1]
-    for copy in started:
-        copy.wait_send()
+    drain()
 
 
 HBM = pl.BlockSpec(memory_space=pltpu.HBM)
@@ -583,8 +605,8 @@
             pltpu.VMEM((RING, depth, 4, 128), F32),
             pltpu.VMEM((RING - 1, depth, 4, 128), F32),
             pltpu.VMEM((RING - 1, CORES, depth - rim, 4, 128), F32),
-            pltpu.VMEM((4, 128), F32),
-            pltpu.VMEM((PLANE - 1, 4, 128), F32),
+            pltpu.VMEM((2, 4, 128), F32),
+            pltpu.VMEM((2, RING, 4, 128), F32),
             pltpu.VMEM((2, CORES, depth, 8, 128), F32),
             pltpu.VMEM((2, CORES, depth, 8, 128), F32),
             pltpu.VMEM((2, CORES, RING, depth * COLBLK, 2, 128), F32),
@@ -602,7 +624,7 @@
             dma((2, 2, nchunk)),
             dma((2, 2, nchunk, RING - 1)),
             dma((2, 2, RING - 1)),
-            dma((2, PLANE - 1)),
+            dma((2, 2, RING)),
             dma((2, CORES, 2, depth)),
             dma((2, CORES, 2, depth)),
             dma((2, 2, nchunk, PLANE - 1)),

time: 74.1 us -> 72.4 us (0.977)
  Pallas kernels: 70.1 us -> 68.4 us
    pallas_call x1, Pallas kernels: 70.1 us -> 68.4 us  [shards(): pl.pallas_call(kernel, out_shape=(jax.ShapeDtypeStruct((2, COLBLK * 128),...]
where the time goes in v5:
time: 72.4 us; the launch traced here: 72.2 us
  Pallas kernels  68.4 us (94%)
  local copies, waits for them, and re-layouts  2.5 us (3%)
  between operations  1.29 us (2%)
    pallas_call x1, Pallas kernels, shards(): pl.pallas_call(kernel, out_shape=(jax.ShapeDtypeStruct((2, COLBLK * 128),...  68.4 us
    unnamed x2, local copies, waits for them, and re-layouts  2.5 us

profile of v5, /device:TPU:1, one launch (start us, length us, event | category | flops | bytes accessed | tf_op | source)
XLA Modules:
  0.0 72.2 jit_solution(697273604726715829)
XLA Ops:
  1.3 68.4 %shard_map.95 = (f32[2,256]{1,0:T(2,128)}, f32[2,512]{1,0:T(2,128)}) custom-call(bf16[1,128,128,128]{3,2,1,0:T(8,128)(2,1)} %tiles_in.1, s32[1,128]{1,0:T(1,128)} %row_in.1, s32[1,128]{1,0:T(1,128)} %col_in.1, s32[1]{0:T(128)S(6)} %copy.12.tile_count, f32[2,256]{1,0:T(2,128)} %cost_in.1, f32[1,512]{1,0:T(1,128)} %bitcast.1, f32[2,256]{1,0:T(2,128)} %x_in.1, ...), custom_call_target="tpu_custom_call" | custom-call | tf_op jit(solution)/shard_map/pallas_call | solution.py:586
  69.7 1.2 %copy.13 = f32[2,256]{1,0:T(2,128)} copy(f32[2,256]{1,0:T(2,128)} %get-tuple-element.4) | data formatting | bytes 4096
  70.9 1.3 %copy.14 = f32[2,512]{1,0:T(2,128)} copy(f32[2,512]{1,0:T(2,128)} %get-tuple-element.5) | data formatting | bytes 8192

commit v6 on v5

--- a/solution.py
+++ b/solution.py
@@ -154,7 +154,7 @@
 ):
     ntile = tiles.shape[0]
     depth = reduced.shape[2]
-    edges = (0, depth // 2 - 1, depth - 3) if depth >= 8 else (0, 1)
+    edges = (0, depth // 2 + 1, depth - 3) if depth >= 8 else (0, 1)
     chunks = tuple(zip(edges[:-1], edges[1:]))
     nchunk = len(chunks)
     rim = edges[-1]
@@ -315,6 +315,7 @@
 
     def reduce_scatter(turn, store, out, from_core, from_y, from_far, combine, steps=None):
         order = tuple(range(nchunk))[::-1]
+        used = pl.ds(0, 4 if steps is not None else 6)
         sent = {}
 
         def send_steps(kind, b):
@@ -335,8 +336,8 @@
             pl.semaphore_wait(barrier, len(peers))
         for b in range(1, RING):
             sent["far", b] = send(
-                out.at[:, b, far],
-                from_far.at[b - 1],
+                out.at[:, b, far, used],
+                from_far.at[b - 1, :, :, used],
                 far_sem.at[turn, 0, b - 1],
                 far_sem.at[turn, 1, b - 1],
                 plane_peer[0, b],
@@ -345,8 +346,8 @@
             at = pl.ds(chunks[n][0], chunks[n][1] - chunks[n][0])
             place_parts(store, *chunks[n])
             sent[n] = send(
-                out.at[1, :, at],
-                from_core.at[:, at],
+                out.at[1, :, at, used],
+                from_core.at[:, at, used],
                 core_sem.at[turn, 0, n],
                 core_sem.at[turn, 1, n],
                 plane_peer[1, 0],
@@ -365,8 +366,8 @@
                 from_core[b, lo:hi] = combine(out[0, b, lo:hi], from_core[b, lo:hi])
             for b in range(1, RING):
                 sent[n, b] = send(
-                    from_core.at[b, at],
-                    from_y.at[b - 1, at],
+                    from_core.at[b, at, used],
+                    from_y.at[b - 1, at, used],
                     ring_sem.at[turn, 0, n, b - 1],
                     ring_sem.at[turn, 1, n, b - 1],
                     plane_peer[0, b],

time: 72.4 us -> 72.2 us (level)
  no operation moved by 1% of the time
where the time goes in v6:
time: 72.2 us; the launch traced here: 72 us
  Pallas kernels  68.3 us (95%)
  local copies, waits for them, and re-layouts  2.5 us (3%)
  between operations  1.29 us (2%)
    pallas_call x1, Pallas kernels, shards(): pl.pallas_call(kernel, out_shape=(jax.ShapeDtypeStruct((2, COLBLK * 128),...  68.3 us
    unnamed x2, local copies, waits for them, and re-layouts  2.5 us

profile of v6, /device:TPU:1, one launch (start us, length us, event | category | flops | bytes accessed | tf_op | source)
XLA Modules:
  0.0 72.0 jit_solution(11999227607175555583)
XLA Ops:
  1.3 68.3 %shard_map.95 = (f32[2,256]{1,0:T(2,128)}, f32[2,512]{1,0:T(2,128)}) custom-call(bf16[1,128,128,128]{3,2,1,0:T(8,128)(2,1)} %tiles_in.1, s32[1,128]{1,0:T(1,128)} %row_in.1, s32[1,128]{1,0:T(1,128)} %col_in.1, s32[1]{0:T(128)S(6)} %copy.12.tile_count, f32[2,256]{1,0:T(2,128)} %cost_in.1, f32[1,512]{1,0:T(1,128)} %bitcast.1, f32[2,256]{1,0:T(2,128)} %x_in.1, ...), custom_call_target="tpu_custom_call" | custom-call | tf_op jit(solution)/shard_map/pallas_call | solution.py:587
  69.5 1.2 %copy.13 = f32[2,256]{1,0:T(2,128)} copy(f32[2,256]{1,0:T(2,128)} %get-tuple-element.4) | data formatting | bytes 4096
  70.8 1.3 %copy.14 = f32[2,512]{1,0:T(2,128)} copy(f32[2,512]{1,0:T(2,128)} %get-tuple-element.5) | data formatting | bytes 8192

commit v7 on v6

--- a/solution.py
+++ b/solution.py
@@ -11,7 +11,7 @@
 RING = 4
 PLANE = CORES * RING
 UNROLL = 64
-PIECE = 64
+PIECE = 16
 
 step_size = 0.0625
 MESH = pl.DeviceIdType.MESH
@@ -237,17 +237,17 @@
     def peak_piece(i, peaks):
         piece_copy(i).wait()
 
-        def peak_body(step, peaks):
+        def peak_body(peaks):
             peaks = list(peaks)
-            for u in range(UNROLL):
-                t = i * PIECE + step * UNROLL + u
+            for u in range(PIECE):
+                t = i * PIECE + u
                 r = live_row(t)
                 size = jnp.abs(tiles[t])
                 for k in range(ROWBLK):
                     peaks[k] = jnp.maximum(peaks[k], jnp.where(r == k, size, jnp.zeros_like(size)))
             return tuple(peaks)
 
-        return lax.fori_loop(0, PIECE // UNROLL, peak_body, peaks)
+        return peak_body(peaks)
 
     peaks = lax.fori_loop(
         0, ntile // PIECE, peak_piece, (jnp.zeros((128, 128), BF16),) * ROWBLK

time: 72.2 us -> 71.5 us (level)
  no operation moved by 1% of the time
where the time goes in v7:
time: 71.5 us; the launch traced here: 71.3 us
  Pallas kernels  67.6 us (95%)
  local copies, waits for them, and re-layouts  2.5 us (3%)
  between operations  1.29 us (2%)
    pallas_call x1, Pallas kernels, shards(): pl.pallas_call(kernel, out_shape=(jax.ShapeDtypeStruct((2, COLBLK * 128),...  67.6 us
    unnamed x2, local copies, waits for them, and re-layouts  2.5 us

profile of v7, /device:TPU:1, one launch (start us, length us, event | category | flops | bytes accessed | tf_op | source)
XLA Modules:
  0.0 71.3 jit_solution(7371771655709685408)
XLA Ops:
  1.3 67.6 %shard_map.95 = (f32[2,256]{1,0:T(2,128)}, f32[2,512]{1,0:T(2,128)}) custom-call(bf16[1,128,128,128]{3,2,1,0:T(8,128)(2,1)} %tiles_in.1, s32[1,128]{1,0:T(1,128)} %row_in.1, s32[1,128]{1,0:T(1,128)} %col_in.1, s32[1]{0:T(128)S(6)} %copy.12.tile_count, f32[2,256]{1,0:T(2,128)} %cost_in.1, f32[1,512]{1,0:T(1,128)} %bitcast.1, f32[2,256]{1,0:T(2,128)} %x_in.1, ...), custom_call_target="tpu_custom_call" | custom-call | tf_op jit(solution)/shard_map/pallas_call | solution.py:587
  68.8 1.2 %copy.13 = f32[2,256]{1,0:T(2,128)} copy(f32[2,256]{1,0:T(2,128)} %get-tuple-element.4) | data formatting | bytes 4096
  70.1 1.3 %copy.14 = f32[2,512]{1,0:T(2,128)} copy(f32[2,512]{1,0:T(2,128)} %get-tuple-element.5) | data formatting | bytes 8192
